TPU v7x, 32 devices: a whole 2x2x4 slice. The times are simulated.
32 devices in a mesh: frame: 8 (over z, y), head: 4 (over x, core).
Axes of the slice: x: 2, y: 2, z: 4, core: 2. Of those that a mesh axis runs over, the one named last changes fastest.
Arguments:
- latents: bfloat16 [4096, 5120], P('frame', 'head'), may hold values from -6 to 6
- queries: bfloat16 [4096, 2560], P('frame', 'head'), may hold values from -22 to 22
- keys: bfloat16 [4096, 2560], P('frame', 'head'), may hold values from -6 to 6
- values: bfloat16 [4096, 2560], P('frame', 'head'), may hold values from -6 to 6
- out_weight: bfloat16 [2560, 5120], P('head'), may hold values from -0.5 to 0.5
- gate_table: float32 [4, 5120], P(None, 'head'), may hold values from 0.5 to 2
- levels: int32 [8], P('frame'), may hold values from 0 to 3
- block_mask: int32 [8, 4], P('frame'), may hold values from 0 to 1, as said below
- fresh: bfloat16 [512, 5120], P(None, 'head'), may hold values from -6 to 6
Outputs:
- velocity: bfloat16 [4096, 5120], P('frame', 'head')
- next_latents: bfloat16 [4096, 5120], P('frame', 'head')
Inputs may be any that keep to these rules, and one draw needn't show every extreme that they name: block_mask[c, 0] is 1 for every span c.
All inputs are finite; a program needn't handle non-finite values.
Results may differ from a plain program's by a relative error of at most 0.012.
Values may be sent and summed in bfloat16 or wider, within the bound.
A program may use at most 128 MiB of HBM per device.

v0:
```python
import math

import jax
import jax.numpy as jnp
from jax import lax
from jax.sharding import PartitionSpec as P

HD = 128
LEVELS = 4


flow_shift = 5.0


def shifted(value, axis, by):
    devices = lax.axis_size(axis)
    pairs = [(i, i + by) for i in range(devices) if 0 <= i + by < devices]
    return lax.ppermute(value, axis, pairs)


def noise_level(point):
    return flow_shift * point / (1.0 + (flow_shift - 1.0) * point)


def shards(latents, queries, keys, values, out_weight, gate_table, levels, block_mask, fresh):
    rows_here = queries.shape[0]
    width_here = queries.shape[1]
    heads_here = width_here // HD
    window = block_mask.shape[1]
    key_list = [keys]
    value_list = [values]
    carried = (keys, values)
    for distance in range(1, window):
        carried = shifted((carried[0], carried[1]), "frame", 1)
        key_list.append(carried[0])
        value_list.append(carried[1])
    key_stack = jnp.stack(key_list, 0)
    value_stack = jnp.stack(value_list, 0)
    position = lax.axis_index("frame")
    distances = jnp.arange(window, dtype=jnp.int32)
    allowed = (block_mask[0] == 1) & (position - distances >= 0)
    scale = 1.0 / math.sqrt(HD)
    query_heads = queries.reshape(rows_here, heads_here, HD)
    key_heads = key_stack.reshape(window, rows_here, heads_here, HD)
    value_heads = value_stack.reshape(window, rows_here, heads_here, HD)
    scores = (
        jnp.einsum("qhd,bkhd->hqbk", query_heads, key_heads, preferred_element_type=jnp.float32)
        * scale
    )
    scores = jnp.where(allowed[None, None, :, None], scores, -jnp.inf)
    top = jnp.max(scores, axis=(2, 3), keepdims=True)
    expd = jnp.exp(scores - top)
    weights = (expd / jnp.sum(expd, axis=(2, 3), keepdims=True)).astype(jnp.bfloat16)
    attended = jnp.einsum(
        "hqbk,bkhd->qhd", weights, value_heads, preferred_element_type=jnp.float32
    )
    attended = attended.reshape(rows_here, width_here).astype(jnp.bfloat16)
    partial_value = jnp.dot(attended, out_weight, preferred_element_type=jnp.float32)
    projected = lax.psum_scatter(
        partial_value.astype(jnp.bfloat16), "head", scatter_dimension=1, tiled=True
    ).astype(jnp.float32)
    level_value = levels[0]
    picker = (jnp.arange(LEVELS, dtype=jnp.int32) == level_value).astype(jnp.float32)
    gate = jnp.dot(picker, gate_table, precision=lax.Precision.HIGHEST)
    level_float = level_value.astype(jnp.float32)
    delta = noise_level(level_float / LEVELS) - noise_level((level_float + 1.0) / LEVELS)
    gated = gate[None, :] * projected
    velocity = gated.astype(jnp.bfloat16)
    update = delta * gated
    updated = (latents.astype(jnp.float32) + update).astype(jnp.bfloat16)
    moved = shifted(updated, "frame", -1)
    is_last = position == lax.axis_size("frame") - 1
    next_latents = jnp.where(is_last, fresh, moved)
    return (velocity, next_latents)


def solution(mesh):
    in_specs = (
        P("frame", "head"),
        P("frame", "head"),
        P("frame", "head"),
        P("frame", "head"),
        P("head", None),
        P(None, "head"),
        P("frame"),
        P("frame", None),
        P(None, "head"),
    )
    out_specs = (P("frame", "head"), P("frame", "head"))
    return jax.shard_map(shards, mesh=mesh, in_specs=in_specs, out_specs=out_specs, check_vma=False)
```

profile of v0, /device:TPU:0, one launch (start us, length us, event | category | flops | bytes accessed | tf_op | source)
XLA Modules:
  0.0 216.2 jit_solution(1556316034301092801)
XLA Ops:
  7.2 0.0 copy-start
  7.2 0.0 copy-start.4
  7.2 0.0 copy-start.6
  7.2 0.0 reduce-scatter.2.cloned.1.call-start
  7.2 1.4 copy.21
  8.6 4.9 %collective-permute-start.3 = (bf16[512,640]{0,1:T(8,128)(2,1)S(1)}, bf16[512,640]{0,1:T(8,128)(2,1)S(1)}, u32[]{:S(2)}, u32[]{:S(2)}) collective-permute-start(bf16[512,640]{0,1:T(8,128)(2,1)S(1)} %copy.21), channel_id=1, source_target_pairs={{0,4},{4,8},{8,12},{12,16},{16,20},{20,24},{24,28},{1,5},{5,9},{9,... | collective-permute-start | bytes 1966088 | tf_op jit(solution)/shard_map/ppermute | solution.py:18
  13.6 4.2 %collective-permute-start = (bf16[512,640]{1,0:T(8,128)(2,1)}, bf16[512,640]{1,0:T(8,128)(2,1)}, u32[]{:S(2)}, u32[]{:S(2)}) collective-permute-start(bf16[512,640]{1,0:T(8,128)(2,1)} %param.12), channel_id=1, source_target_pairs={{0,4},{4,8},{8,12},{12,16},{16,20},{20,24},{24,28},{1,5},{5,9},{9,... | collective-permute-start | bytes 1966088 | tf_op jit(solution)/shard_map/ppermute | solution.py:18
  17.8 10.8 %collective-permute-done.3 = bf16[512,640]{0,1:T(8,128)(2,1)S(1)} collective-permute-done((bf16[512,640]{0,1:T(8,128)(2,1)S(1)}, bf16[512,640]{0,1:T(8,128)(2,1)S(1)}, u32[]{:S(2)}, u32[]{:S(2)}) %collective-permute-start.3) | collective-permute-done | bytes 655392 | tf_op jit(solution)/shard_map/ppermute | solution.py:18
  28.6 0.0 copy-start.5
  28.6 4.4 %collective-permute-start.4 = (bf16[512,640]{0,1:T(8,128)(2,1)S(1)}, bf16[512,640]{0,1:T(8,128)(2,1)S(1)}, u32[]{:S(2)}, u32[]{:S(2)}) collective-permute-start(bf16[512,640]{0,1:T(8,128)(2,1)S(1)} %collective-permute-done.3), channel_id=1, source_target_pairs={{0,4},{4,8},{8,12},{12,16},{16,20},{20,24},{24,28},{1,5},{5,9},{9,... | collective-permute-start | bytes 1966088 | tf_op jit(solution)/shard_map/ppermute | solution.py:18
  33.1 9.7 %collective-permute-done = bf16[512,640]{1,0:T(8,128)(2,1)} collective-permute-done((bf16[512,640]{1,0:T(8,128)(2,1)}, bf16[512,640]{1,0:T(8,128)(2,1)}, u32[]{:S(2)}, u32[]{:S(2)}) %collective-permute-start) | collective-permute-done | bytes 655392 | tf_op jit(solution)/shard_map/ppermute | solution.py:18
  42.8 4.4 %collective-permute-start.1 = (bf16[512,640]{1,0:T(8,128)(2,1)}, bf16[512,640]{1,0:T(8,128)(2,1)S(1)}, u32[]{:S(2)}, u32[]{:S(2)}) collective-permute-start(bf16[512,640]{1,0:T(8,128)(2,1)} %collective-permute-done), channel_id=1, source_target_pairs={{0,4},{4,8},{8,12},{12,16},{16,20},{20,24},{24,28},{1,5},{5,9},{9,... | collective-permute-start | bytes 1966088 | tf_op jit(solution)/shard_map/ppermute | solution.py:18
  47.2 9.5 %collective-permute-done.4 = bf16[512,640]{0,1:T(8,128)(2,1)S(1)} collective-permute-done((bf16[512,640]{0,1:T(8,128)(2,1)S(1)}, bf16[512,640]{0,1:T(8,128)(2,1)S(1)}, u32[]{:S(2)}, u32[]{:S(2)}) %collective-permute-start.4) | collective-permute-done | bytes 655392 | tf_op jit(solution)/shard_map/ppermute | solution.py:18
  56.7 5.2 %collective-permute-start.5 = (bf16[512,640]{0,1:T(8,128)(2,1)S(1)}, bf16[512,640]{0,1:T(8,128)(2,1)}, u32[]{:S(2)}, u32[]{:S(2)}) collective-permute-start(bf16[512,640]{0,1:T(8,128)(2,1)S(1)} %collective-permute-done.4), channel_id=1, source_target_pairs={{0,4},{4,8},{8,12},{12,16},{16,20},{20,24},{24,28},{1,5},{5,9},{9,... | collective-permute-start | bytes 1966088 | tf_op jit(solution)/shard_map/ppermute | solution.py:18
  62.0 0.0 copy-done.5
  62.0 1.3 copy.17
  63.3 1.1 copy.23
  64.4 0.0 copy-done.4
  64.4 1.1 copy.27
  65.5 0.0 copy-done.6
  65.5 2.2 %copy.24 = bf16[1,512,5,128]{3,1,0,2:T(8,128)(2,1)} copy(bf16[1,512,5,128]{1,3,2,0:T(8,128)(2,1)} %bitcast.50) | data formatting | bytes 1310720 | tf_op jit(solution)/shard_map/stack | solution.py:37
  67.7 1.3 copy.18
  69.0 1.1 copy.25
  70.1 0.8 collective-permute-done.1
  70.9 5.1 %collective-permute-start.2 = (bf16[512,640]{1,0:T(8,128)(2,1)S(1)}, bf16[512,640]{1,0:T(8,128)(2,1)}, u32[]{:S(2)}, u32[]{:S(2)}) collective-permute-start(bf16[512,640]{1,0:T(8,128)(2,1)S(1)} %collective-permute-done.1), channel_id=1, source_target_pairs={{0,4},{4,8},{8,12},{12,16},{16,20},{20,24},{24,28},{1,5},{5,9},{9,... | collective-permute-start | bytes 1966088 | tf_op jit(solution)/shard_map/ppermute | solution.py:18
  76.0 0.3 copy.19
  76.3 8.5 %collective-permute-done.5 = bf16[512,640]{0,1:T(8,128)(2,1)} collective-permute-done((bf16[512,640]{0,1:T(8,128)(2,1)S(1)}, bf16[512,640]{0,1:T(8,128)(2,1)}, u32[]{:S(2)}, u32[]{:S(2)}) %collective-permute-start.5) | collective-permute-done | bytes 655392 | tf_op jit(solution)/shard_map/ppermute | solution.py:18
  84.8 1.4 copy.26
  86.2 4.5 %bitcast_reduce_fusion = (f32[5,512]{1,0:T(8,128)S(1)}, f32[5,4,512,512]{3,2,1,0:T(8,128)S(1)}) fusion(pred[4]{0:T(512)(128)(4,1)S(1)} %bitcast_and_fusion, bf16[512,5,128,1]{0,2,3,1:T(8,128)(2,1)} %bitcast.53, bf16[1,512,5,128]{3,1,0,2:T(8,128)(2,1)S(1)} %copy.26, bf16[1,512,5,128]{3,1,0,2:T(8,128)(2,1)} %copy.25, bf16[1,512,5,128]{3,1,0,2:T(8,128)(2,1)} %copy.24, ...), kind=kOutput, calls=%fused_computation.1 | convolution fusion | flops 1361835520 | bytes 24258564 | tf_op jit(solution)/shard_map/qhd,bkhd->hqbk/dot_general | solution.py:47
  90.7 0.0 copy-start.1
  90.8 4.7 %fusion.1 = f32[5,512]{1,0:T(8,128)S(1)} fusion(f32[5,4,512,512]{3,2,1,0:T(8,128)S(1)} %get-tuple-element.5, f32[5,512]{1,0:T(8,128)S(1)} %get-tuple-element.4, pred[4]{0:T(512)(128)(4,1)S(1)} %bitcast_and_fusion), kind=kLoop, calls=%fused_computation.5 | loop fusion | flops 20968960 | bytes 20992004 | tf_op jit(solution)/shard_map/reduce_sum | solution.py:53
  95.4 2.3 %copy-done.1 = f32[5,4,512,512]{3,2,1,0:T(8,128)} copy-done((f32[5,4,512,512]{3,2,1,0:T(8,128)}, f32[5,4,512,512]{3,2,1,0:T(8,128)S(1)}, u32[]{:S(2)}) %copy-start.1) | copy-done | bytes 20971544
  97.7 0.0 collective-permute-done.2
  97.7 1.3 copy.20
  99.1 10.7 %fusion.22 = bf16[5,128,512]{2,1,0:T(8,128)(2,1)S(1)} fusion(f32[5,4,512,512]{3,2,1,0:T(8,128)} %copy-done.1, f32[5,512]{1,0:T(8,128)S(1)} %fusion.1, f32[5,512]{1,0:T(8,128)S(1)} %get-tuple-element.4, pred[4]{0:T(512)(128)(4,1)S(1)} %bitcast_and_fusion, bf16[1,512,5,128]{1,3,0,2:T(8,128)(2,1)S(1)} %bitcast.54, bf16[1,512,5,128]{1,3,0,2:T(8,128)(2,1)S(1)} %bitcast.52, ...), kind=kOutput, calls=%fused_computation.27 | convolution fusion | flops 1372651520 | bytes 24268804 | tf_op jit(solution)/shard_map/hqbk,bkhd->qhd/dot_general | solution.py:54
  109.8 8.9 %convolution_convert_fusion = bf16[512,5120]{1,0:T(8,128)(2,1)} fusion(bf16[512,640]{0,1:T(8,128)(2,1)S(1)} %bitcast.55, bf16[640,5120]{1,0:T(8,128)(2,1)} %param.13), kind=kOutput, calls=%fused_computation.7 | convolution fusion | flops 3358064640 | bytes 12451840 | tf_op jit(solution)/shard_map/dot_general | solution.py:58
  118.7 0.0 copy-start.3
  118.7 0.0 reduce-scatter.2.cloned.1.call-update
  119.5 0.0 copy-done
  119.5 0.2 convolution_reduce_fusion
  119.7 0.0 copy-start.2
  119.7 52.6 %reduce-scatter.2.cloned.1.call-done = bf16[512,1280]{1,0:T(8,128)(2,1)} async-done(((bf16[512,5120]{1,0:T(8,128)(2,1)}), bf16[512,1280]{1,0:T(8,128)(2,1)}) %reduce-scatter.2.cloned.1.call-update) | async-done | bytes 1310736 | tf_op jit(solution)/shard_map/reduce_scatter | solution.py:59
  172.3 0.0 copy-done.3
  172.3 3.3 %add_convert_fusion = (bf16[512,1280]{1,0:T(8,128)(2,1)}, bf16[512,1280]{1,0:T(8,128)(2,1)}) fusion(bf16[512,1280]{1,0:T(8,128)(2,1)S(1)} %copy-done.3, bf16[512,1280]{1,0:T(8,128)(2,1)} %reduce-scatter.2.cloned.1.call-done, f32[]{:T(128)S(6)} %sub.25, f32[1280]{0:T(1024)S(1)} %convolution_reduce_fusion), kind=kLoop, calls=%fused_computation.23 | loop fusion | flops 4587520 | bytes 5248004 | tf_op jit(solution)/shard_map/convert_element_type | solution.py:70
  175.7 1.3 collective-permute-start.6
  177.0 31.2 %collective-permute-done.6 = bf16[512,1280]{1,0:T(8,128)(2,1)S(1)} collective-permute-done((bf16[512,1280]{1,0:T(8,128)(2,1)}, bf16[512,1280]{1,0:T(8,128)(2,1)S(1)}, u32[]{:S(2)}, u32[]{:S(2)}) %collective-permute-start.6) | collective-permute-done | bytes 1310752 | tf_op jit(solution)/shard_map/ppermute | solution.py:18
  208.1 0.0 copy-done.2
  208.1 1.2 broadcast_select_fusion
  (1 shorter events, 0.0 us)
Async XLA Ops:
  7.2 112.4 %copy-start = (f32[4,1280]{1,0:T(4,128)S(1)}, f32[4,1280]{1,0:T(4,128)}, u32[]{:S(2)}) copy-start(f32[4,1280]{1,0:T(4,128)} %param.14) | copy-start | bytes 61444
  7.2 57.2 %copy-start.4 = (bf16[512,640]{1,0:T(8,128)(2,1)S(1)}, bf16[512,640]{1,0:T(8,128)(2,1)}, u32[]{:S(2)}) copy-start(bf16[512,640]{1,0:T(8,128)(2,1)} %param.10) | copy-start | bytes 1966084
  7.2 58.3 %copy-start.6 = (s32[1,4]{1,0:T(1,128)S(1)}, s32[1,4]{1,0:T(1,128)}, u32[]{:S(2)}) copy-start(s32[1,4]{1,0:T(1,128)} %param.16) | copy-start | bytes 52
  7.2 165.1 %reduce-scatter.2.cloned.1.call-start = ((), (), s32[]{:S(2)}) async-start(), calls=%async_computation.1 | async-start | bytes 6553600 | tf_op jit(solution)/shard_map/reduce_scatter | solution.py:59
  8.6 20.0 %collective-permute-start.3 = (bf16[512,640]{0,1:T(8,128)(2,1)S(1)}, bf16[512,640]{0,1:T(8,128)(2,1)S(1)}, u32[]{:S(2)}, u32[]{:S(2)}) collective-permute-start(bf16[512,640]{0,1:T(8,128)(2,1)S(1)} %copy.21), channel_id=1, source_target_pairs={{0,4},{4,8},{8,12},{12,16},{16,20},{20,24},{24,28},{1,5},{5,9},{9,... | collective-permute-start | bytes 1966088 | tf_op jit(solution)/shard_map/ppermute | solution.py:18
  13.6 29.2 %collective-permute-start = (bf16[512,640]{1,0:T(8,128)(2,1)}, bf16[512,640]{1,0:T(8,128)(2,1)}, u32[]{:S(2)}, u32[]{:S(2)}) collective-permute-start(bf16[512,640]{1,0:T(8,128)(2,1)} %param.12), channel_id=1, source_target_pairs={{0,4},{4,8},{8,12},{12,16},{16,20},{20,24},{24,28},{1,5},{5,9},{9,... | collective-permute-start | bytes 1966088 | tf_op jit(solution)/shard_map/ppermute | solution.py:18
  28.6 33.3 %copy-start.5 = (bf16[512,640]{0,1:T(8,128)(2,1)}, bf16[512,640]{0,1:T(8,128)(2,1)S(1)}, u32[]{:S(2)}) copy-start(bf16[512,640]{0,1:T(8,128)(2,1)S(1)} %collective-permute-done.3) | copy-start | bytes 1966084
  28.6 28.1 %collective-permute-start.4 = (bf16[512,640]{0,1:T(8,128)(2,1)S(1)}, bf16[512,640]{0,1:T(8,128)(2,1)S(1)}, u32[]{:S(2)}, u32[]{:S(2)}) collective-permute-start(bf16[512,640]{0,1:T(8,128)(2,1)S(1)} %collective-permute-done.3), channel_id=1, source_target_pairs={{0,4},{4,8},{8,12},{12,16},{16,20},{20,24},{24,28},{1,5},{5,9},{9,... | collective-permute-start | bytes 1966088 | tf_op jit(solution)/shard_map/ppermute | solution.py:18
  42.8 28.1 %collective-permute-start.1 = (bf16[512,640]{1,0:T(8,128)(2,1)}, bf16[512,640]{1,0:T(8,128)(2,1)S(1)}, u32[]{:S(2)}, u32[]{:S(2)}) collective-permute-start(bf16[512,640]{1,0:T(8,128)(2,1)} %collective-permute-done), channel_id=1, source_target_pairs={{0,4},{4,8},{8,12},{12,16},{16,20},{20,24},{24,28},{1,5},{5,9},{9,... | collective-permute-start | bytes 1966088 | tf_op jit(solution)/shard_map/ppermute | solution.py:18
  56.7 28.1 %collective-permute-start.5 = (bf16[512,640]{0,1:T(8,128)(2,1)S(1)}, bf16[512,640]{0,1:T(8,128)(2,1)}, u32[]{:S(2)}, u32[]{:S(2)}) collective-permute-start(bf16[512,640]{0,1:T(8,128)(2,1)S(1)} %collective-permute-done.4), channel_id=1, source_target_pairs={{0,4},{4,8},{8,12},{12,16},{16,20},{20,24},{24,28},{1,5},{5,9},{9,... | collective-permute-start | bytes 1966088 | tf_op jit(solution)/shard_map/ppermute | solution.py:18
  70.9 26.9 %collective-permute-start.2 = (bf16[512,640]{1,0:T(8,128)(2,1)S(1)}, bf16[512,640]{1,0:T(8,128)(2,1)}, u32[]{:S(2)}, u32[]{:S(2)}) collective-permute-start(bf16[512,640]{1,0:T(8,128)(2,1)S(1)} %collective-permute-done.1), channel_id=1, source_target_pairs={{0,4},{4,8},{8,12},{12,16},{16,20},{20,24},{24,28},{1,5},{5,9},{9,... | collective-permute-start | bytes 1966088 | tf_op jit(solution)/shard_map/ppermute | solution.py:18
  90.7 7.0 %copy-start.1 = (f32[5,4,512,512]{3,2,1,0:T(8,128)}, f32[5,4,512,512]{3,2,1,0:T(8,128)S(1)}, u32[]{:S(2)}) copy-start(f32[5,4,512,512]{3,2,1,0:T(8,128)S(1)} %get-tuple-element.5) | copy-start | bytes 62914564
  118.7 53.7 %copy-start.3 = (bf16[512,1280]{1,0:T(8,128)(2,1)S(1)}, bf16[512,1280]{1,0:T(8,128)(2,1)}, u32[]{:S(2)}) copy-start(bf16[512,1280]{1,0:T(8,128)(2,1)} %param.9) | copy-start | bytes 3932164
  119.7 88.4 %copy-start.2 = (bf16[512,1280]{1,0:T(8,128)(2,1)S(1)}, bf16[512,1280]{1,0:T(8,128)(2,1)}, u32[]{:S(2)}) copy-start(bf16[512,1280]{1,0:T(8,128)(2,1)} %param.17) | copy-start | bytes 3932164
  175.7 32.5 %collective-permute-start.6 = (bf16[512,1280]{1,0:T(8,128)(2,1)}, bf16[512,1280]{1,0:T(8,128)(2,1)S(1)}, u32[]{:S(2)}, u32[]{:S(2)}) collective-permute-start(bf16[512,1280]{1,0:T(8,128)(2,1)} %get-tuple-element.2), channel_id=1, source_target_pairs={{4,0},{8,4},{12,8},{16,12},{20,16},{24,20},{28,24},{5,1},{9,5},{13... | collective-permute-start | bytes 3932168 | tf_op jit(solution)/shard_map/ppermute | solution.py:18
Sparse Core Ops, SparseCore 0:
  118.8 53.4 reduce-scatter.1
where the time goes:
time: 217 us; the launch traced here: 216 us
  waiting for transfers between devices  123 us (57%)
  starting transfers between devices  29.7 us (14%)
  matrix products  24.3 us (11%)
  between operations  15 us (7%)
  local copies, waits for them, and re-layouts  14.8 us (7%)
  other arithmetic  9.2 us (4%)
    ppermute x7, waiting for transfers between devices, shifted(): return lax.ppermute(value, axis, pairs)  70.6 us
    reduce_scatter x1, waiting for transfers between devices, shards(): lax.psum_scatter(partial_value.astype(jnp.bfloat16), 'head', scatter_dime...  52.6 us
    ppermute x7, starting transfers between devices, shifted(): return lax.ppermute(value, axis, pairs)  29.6 us
    dot_general x1, matrix products, shards(): jnp.einsum('hqbk,bkhd->qhd', weights, value_heads, preferred_element_type...  10.7 us
    dot_general x1, matrix products, shards(): jnp.dot(attended, out_weight, preferred_element_type=jnp.float32)  8.9 us
    unnamed x17, local copies, waits for them, and re-layouts  6.15 us
    another operation x4, local copies, waits for them, and re-layouts, shards(): key_stack = jnp.stack(key_list, 0)  5.76 us
    reduce_sum x1, other arithmetic, shards(): jnp.sum(expd, axis=(2, 3), keepdims=True)  4.67 us
  transfers between devices with their start and end apart: 8, of which 7 were waited for; matrix products, arithmetic and copies ran while one was open for 9% of the time, Pallas kernels for 0%

commit v1 on v0

v1 whole, which is shorter than its diff:
```python
import functools
import math

import jax
import jax.numpy as jnp
from jax import lax
from jax.experimental import pallas as pl
from jax.experimental.pallas import tpu as pltpu
from jax.sharding import PartitionSpec as P


HD = 128
LEVELS = 4
CHUNKS = 4
MASKED = -1e30


flow_shift = 5.0


def shifted(value, axis, by):
    devices = lax.axis_size(axis)
    pairs = [(i, i + by) for i in range(devices) if 0 <= i + by < devices]
    return lax.ppermute(value, axis, pairs)


def swapped(value, axis, bit):
    devices = lax.axis_size(axis)
    return lax.ppermute(value, axis, [(i, i ^ bit) for i in range(devices)])


def noise_level(point):
    return flow_shift * point / (1.0 + (flow_shift - 1.0) * point)


def weights_kernel(blocks, flag_ref, q_ref, *refs):
    k_refs, v_refs = refs[:blocks], refs[blocks:2 * blocks - 1]
    acc_ref, weight_ref = refs[2 * blocks - 1:]
    query = q_ref[...]
    scale = math.log2(math.e) / math.sqrt(HD)
    scores = []
    for b in range(blocks):
        raw = lax.dot_general(
            query, k_refs[b][...], (((1,), (1,)), ((), ())), preferred_element_type=jnp.float32
        )
        scores.append(jnp.where(flag_ref[b] != 0, raw * scale, MASKED))
    top = functools.reduce(jnp.maximum, [jnp.max(s, axis=1, keepdims=True) for s in scores])
    expd = [jnp.exp2(s - top) for s in scores]
    total = sum(jnp.sum(e, axis=1, keepdims=True) for e in expd)
    inverse = 1.0 / total
    acc = sum(
        jnp.dot(expd[b].astype(jnp.bfloat16), v_refs[b][...], preferred_element_type=jnp.float32)
        for b in range(blocks - 1)
    )
    acc_ref[...] = acc * inverse
    weight_ref[...] = (expd[-1] * inverse).astype(jnp.bfloat16)


def finish_kernel(weight_ref, v_ref, acc_ref, out_ref):
    last = jnp.dot(weight_ref[...], v_ref[...], preferred_element_type=jnp.float32)
    out_ref[...] = (acc_ref[...] + last).astype(jnp.bfloat16)


def attention(flags, query, key_list, value_list):
    rows, width = query.shape
    heads = width // HD
    blocks = len(key_list)
    span = key_list[0].shape[0]
    column = pl.BlockSpec((rows, HD), lambda h: (0, h))
    key_column = pl.BlockSpec((span, HD), lambda h: (0, h))
    weight_block = pl.BlockSpec((rows, span), lambda h: (h, 0))
    params = pltpu.CompilerParams(vmem_limit_bytes=40 * 1024 * 1024)
    acc, weights = pl.pallas_call(
        functools.partial(weights_kernel, blocks),
        grid=(heads,),
        in_specs=[pl.BlockSpec(memory_space=pltpu.SMEM), column] + [key_column] * (2 * blocks - 1),
        out_specs=[column, weight_block],
        out_shape=[
            jax.ShapeDtypeStruct((rows, width), jnp.float32),
            jax.ShapeDtypeStruct((heads * rows, span), jnp.bfloat16),
        ],
        cost_estimate=pl.CostEstimate(
            flops=16 * rows * width * span * blocks,
            bytes_accessed=4 * blocks * rows * width * 2,
            transcendentals=heads * rows * span * blocks,
        ),
        compiler_params=params,
    )(flags, query, *key_list, *value_list[:-1])
    return pl.pallas_call(
        finish_kernel,
        grid=(heads,),
        in_specs=[weight_block, key_column, column],
        out_specs=column,
        out_shape=jax.ShapeDtypeStruct((rows, width), jnp.bfloat16),
        cost_estimate=pl.CostEstimate(
            flops=2 * rows * width * span, bytes_accessed=8 * rows * width, transcendentals=0
        ),
        compiler_params=params,
    )(weights, value_list[-1], acc)


def shards(latents, queries, keys, values, out_weight, gate_table, levels, block_mask, fresh):
    window = block_mask.shape[1]
    position = lax.axis_index("frame")
    frames = lax.axis_size("frame")
    distances = jnp.arange(window, dtype=jnp.int32)
    allowed = ((block_mask[0] == 1) & (position - distances >= 0)).astype(jnp.int32)

    key_at = {0: keys}
    value_at = {0: values}
    if frames % 2 == 0 and window == 4:
        odd = position % 2 == 1
        key_at[2] = shifted(keys, "frame", 2)
        value_at[2] = shifted(values, "frame", 2)
        key_at[1] = swapped(jnp.where(odd, key_at[2], keys), "frame", 1)
        value_at[1] = swapped(jnp.where(odd, value_at[2], values), "frame", 1)
        key_at[3] = shifted(key_at[1], "frame", 2)
        value_at[3] = shifted(value_at[1], "frame", 2)
    else:
        for distance in range(1, window):
            key_at[distance] = shifted(key_at[distance - 1], "frame", 1)
            value_at[distance] = shifted(value_at[distance - 1], "frame", 1)

    f32 = jnp.float32
    attended = attention(
        allowed, queries, [key_at[d] for d in range(window)], [value_at[d] for d in range(window)]
    )

    level_value = levels[0]
    picker = (jnp.arange(LEVELS, dtype=jnp.int32) == level_value).astype(f32)
    gate = jnp.dot(picker, gate_table, precision=lax.Precision.HIGHEST)
    level_float = level_value.astype(f32)
    delta = noise_level(level_float / LEVELS) - noise_level((level_float + 1.0) / LEVELS)
    is_last = position == frames - 1

    rows = queries.shape[0]
    out_width = latents.shape[1]
    heads = lax.axis_size("head")
    me = lax.axis_index("head")
    step = rows // CHUNKS
    bf16 = jnp.bfloat16
    parts = [slice(chunk * step, (chunk + 1) * step) for chunk in range(CHUNKS)]

    def project(owner):
        weight = lax.dynamic_slice_in_dim(out_weight, owner * out_width, out_width, 1)
        return jnp.dot(attended, weight, preferred_element_type=f32).astype(bf16)

    if heads == 4:
        for_pair = project(me ^ 3)
        from_pair = [swapped(for_pair[here], "head", 1) for here in parts]
        for_far = project(me ^ 2)
        from_far = [
            swapped((for_far[here].astype(f32) + from_pair[chunk].astype(f32)).astype(bf16), "head", 2)
            for chunk, here in enumerate(parts)
        ]
        for_near = project(me ^ 1)
        from_near = [swapped(for_near[here], "head", 1) for here in parts]
        own = project(me)
    else:
        whole = jnp.dot(attended, out_weight, preferred_element_type=f32).astype(bf16)
        own = lax.psum_scatter(whole, "head", scatter_dimension=1, tiled=True)
    velocities = []
    moves = []
    before = None
    for chunk, here in enumerate(parts):
        projected = own[here].astype(f32)
        if heads == 4:
            far = from_far[chunk]
            if before is not None:
                far, _ = lax.optimization_barrier((far, before))
            projected = projected + from_near[chunk].astype(f32) + far.astype(f32)
        gated = gate[None, :] * projected
        velocities.append(gated.astype(bf16))
        updated = (latents[here].astype(f32) + delta * gated).astype(bf16)
        moves.append(shifted(updated, "frame", -1))
        before = updated
    next_latents = jnp.where(is_last, fresh, jnp.concatenate(moves, 0))
    return (jnp.concatenate(velocities, 0), next_latents)


def solution(mesh):
    in_specs = (
        P("frame", "head"),
        P("frame", "head"),
        P("frame", "head"),
        P("frame", "head"),
        P("head", None),
        P(None, "head"),
        P("frame"),
        P("frame", None),
        P(None, "head"),
    )
    out_specs = (P("frame", "head"), P("frame", "head"))

    return jax.shard_map(shards, mesh=mesh, in_specs=in_specs, out_specs=out_specs, check_vma=False)
```

time: 217 us -> 146 us (0.67)
  waiting for transfers between devices: 123 us -> 77.7 us
  matrix products: 24.3 us -> 8.07 us
  Pallas kernels: 0 us -> 15.3 us
  local copies, waits for them, and re-layouts: 14.8 us -> 0.23 us
  between operations: 15 us -> 1.71 us
  starting transfers between devices: 29.7 us -> 32.3 us
    reduce_scatter x1 -> x0, waiting for transfers between devices: 52.6 us -> none  [shards(): lax.psum_scatter(partial_value.astype(jnp.bfloat16), 'head', scatter_dime...]
    ppermute x0 -> x14, waiting for transfers between devices: none -> 28.5 us  [swapped(): return lax.ppermute(value, axis, [(i, i ^ bit) for i in range(devices)])]
    ppermute x7 -> x8, waiting for transfers between devices: 70.6 us -> 49.2 us  [shifted(): return lax.ppermute(value, axis, pairs)]
    dot_general x3 -> x4, matrix products: 24.1 us -> 7.91 us  [project(): return jnp.dot(attended, weight, preferred_element_type=f32).astype(bf16)]
    pallas_call x0 -> x2, Pallas kernels: none -> 15.3 us  [the longest x1 13.5 us: attention(): pl.pallas_call(functools.partial(weights_kernel, blocks), grid=(heads,),...]
    ppermute x0 -> x14, starting transfers between devices: none -> 9.06 us  [swapped(): return lax.ppermute(value, axis, [(i, i ^ bit) for i in range(devices)])]
    ppermute x7 -> x8, starting transfers between devices: 29.6 us -> 23.2 us  [shifted(): return lax.ppermute(value, axis, pairs)]
    unnamed x17 -> x20, local copies, waits for them, and re-layouts: 6.15 us -> 0.05 us
  transfers between devices with their start and end apart: 8 -> 22, of which waited for: 7 -> 12; matrix products, arithmetic and copies ran while one was open for 9% -> 9% of each run, Pallas kernels for 0% -> 9%
where the time goes in v1:
time: 146 us
  waiting for transfers between devices  77.7 us (53%)
  starting transfers between devices  32.3 us (22%)
  Pallas kernels  15.3 us (10%)
  other arithmetic  10.7 us (7%)
  matrix products  8.07 us (6%)
  between operations  1.71 us (1%)
    ppermute x8, waiting for transfers between devices, shifted(): return lax.ppermute(value, axis, pairs)  49.2 us
    ppermute x14, waiting for transfers between devices, swapped(): return lax.ppermute(value, axis, [(i, i ^ bit) for i in range(devices)])  28.5 us
    ppermute x8, starting transfers between devices, shifted(): return lax.ppermute(value, axis, pairs)  23.2 us
    pallas_call x1, Pallas kernels, attention(): pl.pallas_call(functools.partial(weights_kernel, blocks), grid=(heads,),...  13.5 us
    ppermute x14, starting transfers between devices, swapped(): return lax.ppermute(value, axis, [(i, i ^ bit) for i in range(devices)])  9.06 us
    dot_general x4, matrix products, project(): return jnp.dot(attended, weight, preferred_element_type=f32).astype(bf16)  7.91 us
  transfers between devices with their start and end apart: 22, of which 12 were waited for; matrix products, arithmetic and copies ran while one was open for 9% of the time, Pallas kernels for 9%

profile of v1, /device:TPU:0, one launch (start us, length us, event | category | flops | bytes accessed | tf_op | source)
XLA Modules:
  0.0 145.9 jit_solution(9612513572043395889)
XLA Ops:
  0.7 5.1 %collective-permute-start = (bf16[512,640]{1,0:T(8,128)(2,1)}, bf16[512,640]{1,0:T(8,128)(2,1)S(1)}, u32[]{:S(2)}, u32[]{:S(2)}) collective-permute-start(bf16[512,640]{1,0:T(8,128)(2,1)} %refs_0_.1), channel_id=1, source_target_pairs={{0,8},{4,12},{8,16},{12,20},{16,24},{20,28},{1,9},{5,13},{9,17},{1... | collective-permute-start | bytes 1966088 | tf_op jit(solution)/shard_map/ppermute | solution.py:24
  5.8 3.5 %collective-permute-start.3 = (bf16[512,640]{1,0:T(8,128)(2,1)}, bf16[512,640]{1,0:T(8,128)(2,1)S(1)}, u32[]{:S(2)}, u32[]{:S(2)}) collective-permute-start(bf16[512,640]{1,0:T(8,128)(2,1)} %refs_4_.1), channel_id=1, source_target_pairs={{0,8},{4,12},{8,16},{12,20},{16,24},{20,28},{1,9},{5,13},{9,17},{1... | collective-permute-start | bytes 1966088 | tf_op jit(solution)/shard_map/ppermute | solution.py:24
  9.3 11.8 %collective-permute-done.refs_2_ = bf16[512,640]{1,0:T(8,128)(2,1)S(1)} collective-permute-done((bf16[512,640]{1,0:T(8,128)(2,1)}, bf16[512,640]{1,0:T(8,128)(2,1)S(1)}, u32[]{:S(2)}, u32[]{:S(2)}) %collective-permute-start) | collective-permute-done | bytes 655392 | tf_op jit(solution)/shard_map/ppermute | solution.py:24
  21.2 1.2 broadcast_select_fusion.1
  22.4 0.5 collective-permute-start.1
  22.9 11.2 %collective-permute-done.3.refs_6_ = bf16[512,640]{1,0:T(8,128)(2,1)S(1)} collective-permute-done((bf16[512,640]{1,0:T(8,128)(2,1)}, bf16[512,640]{1,0:T(8,128)(2,1)S(1)}, u32[]{:S(2)}, u32[]{:S(2)}) %collective-permute-start.3) | collective-permute-done | bytes 655392 | tf_op jit(solution)/shard_map/ppermute | solution.py:24
  34.1 0.9 broadcast_select_fusion
  35.0 1.5 %collective-permute-start.4 = (bf16[512,640]{1,0:T(8,128)(2,1)}, bf16[512,640]{1,0:T(8,128)(2,1)}, u32[]{:S(2)}, u32[]{:S(2)}) collective-permute-start(bf16[512,640]{1,0:T(8,128)(2,1)} %broadcast_select_fusion), channel_id=1, source_target_pairs={{0,4},{4,0},{8,12},{12,8},{16,20},{20,16},{24,28},{28,24},{1,5},{5... | collective-permute-start | bytes 1966088 | tf_op jit(solution)/shard_map/ppermute | solution.py:29
  36.5 0.6 collective-permute-done.1.refs_1_
  37.1 5.0 %collective-permute-start.2 = (bf16[512,640]{1,0:T(8,128)(2,1)}, bf16[512,640]{1,0:T(8,128)(2,1)}, u32[]{:S(2)}, u32[]{:S(2)}) collective-permute-start(bf16[512,640]{1,0:T(8,128)(2,1)} %collective-permute-done.1.refs_1_), channel_id=1, source_target_pairs={{0,8},{4,12},{8,16},{12,20},{16,24},{20,28},{1,9},{5,13},{9,17},{1... | collective-permute-start | bytes 1966088 | tf_op jit(solution)/shard_map/ppermute | solution.py:24
  42.8 8.2 %collective-permute-done.4.refs_5_ = bf16[512,640]{1,0:T(8,128)(2,1)} collective-permute-done((bf16[512,640]{1,0:T(8,128)(2,1)}, bf16[512,640]{1,0:T(8,128)(2,1)}, u32[]{:S(2)}, u32[]{:S(2)}) %collective-permute-start.4) | collective-permute-done | bytes 655392 | tf_op jit(solution)/shard_map/ppermute | solution.py:29
  51.1 4.3 %collective-permute-start.5 = (bf16[512,640]{1,0:T(8,128)(2,1)}, bf16[512,640]{1,0:T(8,128)(2,1)S(1)}, u32[]{:S(2)}, u32[]{:S(2)}) collective-permute-start(bf16[512,640]{1,0:T(8,128)(2,1)} %collective-permute-done.4.refs_5_), channel_id=1, source_target_pairs={{0,8},{4,12},{8,16},{12,20},{16,24},{20,28},{1,9},{5,13},{9,17},{1... | collective-permute-start | bytes 1966088 | tf_op jit(solution)/shard_map/ppermute | solution.py:24
  55.4 13.5 %shard_map.104 = (f32[512,640]{1,0:T(8,128)S(1)}, bf16[2560,512]{1,0:T(8,128)(2,1)S(1)}) custom-call(s32[4]{0:T(128)S(1)} %fusion.8.flag_ref, bf16[512,640]{1,0:T(8,128)(2,1)S(1)} %copy-done.3, bf16[512,640]{1,0:T(8,128)(2,1)S(1)} %copy-done.1, bf16[512,640]{1,0:T(8,128)(2,1)} %collective-permute-done.1.refs_1_, ...), custom_call_target="tpu_custom_call" | custom-call | flops 10737418240 | bytes 10485760 | tf_op jit(solution)/shard_map/pallas_call | solution.py:73
  68.9 1.8 %shard_map.105 = bf16[512,640]{1,0:T(8,128)(2,1)S(1)} custom-call(bf16[2560,512]{1,0:T(8,128)(2,1)S(1)} %get-tuple-element.7.weight_ref, bf16[512,640]{1,0:T(8,128)(2,1)S(1)} %collective-permute-done.5.v_ref, f32[512,640]{1,0:T(8,128)S(1)} %get-tuple-element.8.acc_ref), custom_call_target="tpu_custom_call" | custom-call | flops 335544320 | bytes 2621440 | tf_op jit(solution)/shard_map/pallas_call | solution.py:89
  70.8 2.8 %convolution_convert_fusion = bf16[512,1280]{1,0:T(8,128)(2,1)S(1)} fusion(bf16[512,640]{1,0:T(8,128)(2,1)S(1)} %shard_map.105, bf16[640,5120]{1,0:T(8,128)(2,1)} %param.13, s32[]{:T(128)S(6)} %select_n.46), kind=kOutput, calls=%fused_computation | convolution fusion | flops 839516160 | bytes 3604484 | tf_op jit(solution)/shard_map/dot_general | solution.py:146
  73.7 0.5 collective-permute-start.13
  74.3 0.4 collective-permute-start.7
  74.7 1.2 convolution_convert_fusion.2
  76.0 0.1 collective-permute-start.6
  76.2 1.2 convolution_convert_fusion.1
  77.4 1.1 add_convert_fusion.7
  78.6 1.5 %collective-permute-start.8 = (bf16[128,1280]{1,0:T(8,128)(2,1)}, bf16[128,1280]{1,0:T(8,128)(2,1)S(1)}, u32[]{:S(2)}, u32[]{:S(2)}) collective-permute-start(bf16[128,1280]{1,0:T(8,128)(2,1)} %get-tuple-element.24), channel_id=1, source_target_pairs={{0,2},{1,3},{2,0},{3,1},{4,6},{5,7},{6,4},{7,5},{8,10},{9,11},{10,... | collective-permute-start | bytes 983048 | tf_op jit(solution)/shard_map/ppermute | solution.py:29
  80.1 0.2 convolution_reduce_fusion
  80.3 0.2 collective-permute-start.9
  80.6 0.3 collective-permute-start.12
  80.9 0.2 collective-permute-start.15
  81.1 2.7 %convolution_convert_fusion.3 = bf16[512,1280]{1,0:T(8,128)(2,1)S(1)} fusion(bf16[512,640]{1,0:T(8,128)(2,1)S(1)} %shard_map.105, bf16[640,5120]{1,0:T(8,128)(2,1)} %param.13, s32[]{:T(128)S(6)} %select_n.43), kind=kOutput, calls=%fused_computation.3 | convolution fusion | flops 839516160 | bytes 3604484 | tf_op jit(solution)/shard_map/dot_general | solution.py:146
  83.8 0.6 collective-permute-start.11
  84.4 4.9 %collective-permute-done.8 = bf16[128,1280]{1,0:T(8,128)(2,1)S(1)} collective-permute-done((bf16[128,1280]{1,0:T(8,128)(2,1)}, bf16[128,1280]{1,0:T(8,128)(2,1)S(1)}, u32[]{:S(2)}, u32[]{:S(2)}) %collective-permute-start.8) | collective-permute-done | bytes 327712 | tf_op jit(solution)/shard_map/ppermute | solution.py:29
  89.4 1.5 %collective-permute-start.14 = (bf16[128,1280]{1,0:T(8,128)(2,1)S(1)}, bf16[128,1280]{1,0:T(8,128)(2,1)S(1)}, u32[]{:S(2)}, u32[]{:S(2)}) collective-permute-start(bf16[128,1280]{1,0:T(8,128)(2,1)S(1)} %get-tuple-element.26), channel_id=1, source_target_pairs={{0,2},{1,3},{2,0},{3,1},{4,6},{5,7},{6,4},{7,5},{8,10},{9,11},{10,... | collective-permute-start | bytes 983048 | tf_op jit(solution)/shard_map/ppermute | solution.py:29
  90.9 1.0 fusion.4
  91.8 4.6 %collective-permute-done.11 = bf16[128,1280]{1,0:T(8,128)(2,1)S(1)} collective-permute-done((bf16[128,1280]{1,0:T(8,128)(2,1)S(1)}, bf16[128,1280]{1,0:T(8,128)(2,1)S(1)}, u32[]{:S(2)}, u32[]{:S(2)}) %collective-permute-start.11) | collective-permute-done | bytes 327712 | tf_op jit(solution)/shard_map/ppermute | solution.py:29
  96.4 1.5 %collective-permute-start.17 = (bf16[128,1280]{1,0:T(8,128)(2,1)S(1)}, bf16[128,1280]{1,0:T(8,128)(2,1)S(1)}, u32[]{:S(2)}, u32[]{:S(2)}) collective-permute-start(bf16[128,1280]{1,0:T(8,128)(2,1)S(1)} %get-tuple-element.25), channel_id=1, source_target_pairs={{0,2},{1,3},{2,0},{3,1},{4,6},{5,7},{6,4},{7,5},{8,10},{9,11},{10,... | collective-permute-start | bytes 983048 | tf_op jit(solution)/shard_map/ppermute | solution.py:29
  97.9 1.0 fusion.5
  98.8 4.6 %collective-permute-done.14 = bf16[128,1280]{1,0:T(8,128)(2,1)S(1)} collective-permute-done((bf16[128,1280]{1,0:T(8,128)(2,1)S(1)}, bf16[128,1280]{1,0:T(8,128)(2,1)S(1)}, u32[]{:S(2)}, u32[]{:S(2)}) %collective-permute-start.14) | collective-permute-done | bytes 327712 | tf_op jit(solution)/shard_map/ppermute | solution.py:29
  103.4 1.0 fusion.6
  104.4 5.5 %collective-permute-done.17 = bf16[128,1280]{1,0:T(8,128)(2,1)S(1)} collective-permute-done((bf16[128,1280]{1,0:T(8,128)(2,1)S(1)}, bf16[128,1280]{1,0:T(8,128)(2,1)S(1)}, u32[]{:S(2)}, u32[]{:S(2)}) %collective-permute-start.17) | collective-permute-done | bytes 327712 | tf_op jit(solution)/shard_map/ppermute | solution.py:29
  109.9 1.0 add_convert_fusion
  110.9 1.4 collective-permute-start.21
  112.3 1.3 collective-permute-start.20
  113.6 1.3 collective-permute-start.19
  114.9 1.3 collective-permute-start.18
  116.2 1.1 pad_maximum_fusion
  117.3 6.3 %collective-permute-done.21 = bf16[128,1280]{1,0:T(8,128)(2,1)S(1)} collective-permute-done((bf16[128,1280]{1,0:T(8,128)(2,1)}, bf16[128,1280]{1,0:T(8,128)(2,1)S(1)}, u32[]{:S(2)}, u32[]{:S(2)}) %collective-permute-start.21) | collective-permute-done | bytes 327712 | tf_op jit(solution)/shard_map/ppermute | solution.py:24
  123.7 7.0 %collective-permute-done.20 = bf16[128,1280]{1,0:T(8,128)(2,1)S(1)} collective-permute-done((bf16[128,1280]{1,0:T(8,128)(2,1)}, bf16[128,1280]{1,0:T(8,128)(2,1)S(1)}, u32[]{:S(2)}, u32[]{:S(2)}) %collective-permute-start.20) | collective-permute-done | bytes 327712 | tf_op jit(solution)/shard_map/ppermute | solution.py:24
  130.7 7.1 %collective-permute-done.19 = bf16[128,1280]{1,0:T(8,128)(2,1)} collective-permute-done((bf16[128,1280]{1,0:T(8,128)(2,1)}, bf16[128,1280]{1,0:T(8,128)(2,1)}, u32[]{:S(2)}, u32[]{:S(2)}) %collective-permute-start.19) | collective-permute-done | bytes 327712 | tf_op jit(solution)/shard_map/ppermute | solution.py:24
  137.8 5.7 %collective-permute-done.18 = bf16[128,1280]{1,0:T(8,128)(2,1)} collective-permute-done((bf16[128,1280]{1,0:T(8,128)(2,1)}, bf16[128,1280]{1,0:T(8,128)(2,1)}, u32[]{:S(2)}, u32[]{:S(2)}) %collective-permute-start.18) | collective-permute-done | bytes 327712 | tf_op jit(solution)/shard_map/ppermute | solution.py:24
  143.5 2.4 %maximum_select_fusion = bf16[512,1280]{1,0:T(8,128)(2,1)} fusion(bf16[512,1280]{1,0:T(8,128)(2,1)S(1)} %copy-done.4, bf16[128,1280]{1,0:T(8,128)(2,1)S(1)} %collective-permute-done.21, bf16[128,1280]{1,0:T(8,128)(2,1)S(1)} %collective-permute-done.20, bf16[128,1280]{1,0:T(8,128)(2,1)} %collective-permute-done.19, ...), kind=kLoop, calls=%fused_computation.9 | loop fusion | flops 5898240 | bytes 3932161 | tf_op jit(solution)/shard_map/jit(_where)/select_n | solution.py:177
  (36 shorter events, 0.4 us)
Async XLA Ops:
  0.6 79.4 %copy-start = (f32[4,1280]{1,0:T(4,128)S(1)}, f32[4,1280]{1,0:T(4,128)}, u32[]{:S(2)}) copy-start(f32[4,1280]{1,0:T(4,128)} %param.14) | copy-start | bytes 61444
  0.6 33.4 %copy-start.2 = (bf16[512,640]{1,0:T(8,128)(2,1)S(1)}, bf16[512,640]{1,0:T(8,128)(2,1)}, u32[]{:S(2)}) copy-start(bf16[512,640]{1,0:T(8,128)(2,1)} %refs_4_.1) | copy-start | bytes 1966084
  0.7 20.5 %collective-permute-start = (bf16[512,640]{1,0:T(8,128)(2,1)}, bf16[512,640]{1,0:T(8,128)(2,1)S(1)}, u32[]{:S(2)}, u32[]{:S(2)}) collective-permute-start(bf16[512,640]{1,0:T(8,128)(2,1)} %refs_0_.1), channel_id=1, source_target_pairs={{0,8},{4,12},{8,16},{12,20},{16,24},{20,28},{1,9},{5,13},{9,17},{1... | collective-permute-start | bytes 1966088 | tf_op jit(solution)/shard_map/ppermute | solution.py:24
  5.8 28.3 %collective-permute-start.3 = (bf16[512,640]{1,0:T(8,128)(2,1)}, bf16[512,640]{1,0:T(8,128)(2,1)S(1)}, u32[]{:S(2)}, u32[]{:S(2)}) collective-permute-start(bf16[512,640]{1,0:T(8,128)(2,1)} %refs_4_.1), channel_id=1, source_target_pairs={{0,8},{4,12},{8,16},{12,20},{16,24},{20,28},{1,9},{5,13},{9,17},{1... | collective-permute-start | bytes 1966088 | tf_op jit(solution)/shard_map/ppermute | solution.py:24
  9.3 33.5 %copy-start.7 = (s32[1,4]{1,0:T(1,128)S(1)}, s32[1,4]{1,0:T(1,128)}, u32[]{:S(2)}) copy-start(s32[1,4]{1,0:T(1,128)} %param.16) | copy-start | bytes 52
  9.3 46.1 %copy-start.1 = (bf16[512,640]{1,0:T(8,128)(2,1)S(1)}, bf16[512,640]{1,0:T(8,128)(2,1)}, u32[]{:S(2)}) copy-start(bf16[512,640]{1,0:T(8,128)(2,1)} %refs_0_.1) | copy-start | bytes 1966084
  9.3 46.1 %copy-start.3 = (bf16[512,640]{1,0:T(8,128)(2,1)S(1)}, bf16[512,640]{1,0:T(8,128)(2,1)}, u32[]{:S(2)}) copy-start(bf16[512,640]{1,0:T(8,128)(2,1)} %q_ref.1) | copy-start | bytes 1966084
  22.4 14.8 %collective-permute-start.1 = (bf16[512,640]{1,0:T(8,128)(2,1)S(1)}, bf16[512,640]{1,0:T(8,128)(2,1)}, u32[]{:S(2)}, u32[]{:S(2)}) collective-permute-start(bf16[512,640]{1,0:T(8,128)(2,1)S(1)} %broadcast_select_fusion.1), channel_id=1, source_target_pairs={{0,4},{4,0},{8,12},{12,8},{16,20},{20,16},{24,28},{28,24},{1,5},{5... | collective-permute-start | bytes 1966088 | tf_op jit(solution)/shard_map/ppermute | solution.py:29
  35.0 16.1 %collective-permute-start.4 = (bf16[512,640]{1,0:T(8,128)(2,1)}, bf16[512,640]{1,0:T(8,128)(2,1)}, u32[]{:S(2)}, u32[]{:S(2)}) collective-permute-start(bf16[512,640]{1,0:T(8,128)(2,1)} %broadcast_select_fusion), channel_id=1, source_target_pairs={{0,4},{4,0},{8,12},{12,8},{16,20},{20,16},{24,28},{28,24},{1,5},{5... | collective-permute-start | bytes 1966088 | tf_op jit(solution)/shard_map/ppermute | solution.py:29
  37.1 18.2 %collective-permute-start.2 = (bf16[512,640]{1,0:T(8,128)(2,1)}, bf16[512,640]{1,0:T(8,128)(2,1)}, u32[]{:S(2)}, u32[]{:S(2)}) collective-permute-start(bf16[512,640]{1,0:T(8,128)(2,1)} %collective-permute-done.1.refs_1_), channel_id=1, source_target_pairs={{0,8},{4,12},{8,16},{12,20},{16,24},{20,28},{1,9},{5,13},{9,17},{1... | collective-permute-start | bytes 1966088 | tf_op jit(solution)/shard_map/ppermute | solution.py:24
  51.1 17.8 %collective-permute-start.5 = (bf16[512,640]{1,0:T(8,128)(2,1)}, bf16[512,640]{1,0:T(8,128)(2,1)S(1)}, u32[]{:S(2)}, u32[]{:S(2)}) collective-permute-start(bf16[512,640]{1,0:T(8,128)(2,1)} %collective-permute-done.4.refs_5_), channel_id=1, source_target_pairs={{0,8},{4,12},{8,16},{12,20},{16,24},{20,28},{1,9},{5,13},{9,17},{1... | collective-permute-start | bytes 1966088 | tf_op jit(solution)/shard_map/ppermute | solution.py:24
  68.9 5.8 %slice-start = ((s8[6553600]{0:T(1024)(128)(4,1)}), s8[2359296]{0:T(1024)(128)(4,1)S(1)}, s32[]{:S(2)}) async-start(s8[6553600]{0:T(1024)(128)(4,1)} %bitcast.15), calls=%async_computation | async-start | bytes 4718592
  70.7 4.0 %slice-start.1 = ((s8[6553600]{0:T(1024)(128)(4,1)}), s8[4194304]{0:T(1024)(128)(4,1)S(1)}, s32[]{:S(2)}) async-start(s8[6553600]{0:T(1024)(128)(4,1)} %bitcast.15), calls=%async_computation.1 | async-start | bytes 8388608
  73.6 3.7 %collective-permute-start.10 = (bf16[128,1280]{1,0:T(8,128)(2,1)S(1)}, bf16[128,1280]{1,0:T(8,128)(2,1)S(1)}, u32[]{:S(2)}, u32[]{:S(2)}) collective-permute-start(bf16[128,1280]{1,0:T(8,128)(2,1)S(1)} %get-tuple-element.31), channel_id=1, source_target_pairs={{0,1},{1,0},{2,3},{3,2},{4,5},{5,4},{6,7},{7,6},{8,9},{9,8},{10,11... | collective-permute-start | bytes 983048 | tf_op jit(solution)/shard_map/ppermute | solution.py:29
  73.7 3.7 %collective-permute-start.13 = (bf16[128,1280]{1,0:T(8,128)(2,1)S(1)}, bf16[128,1280]{1,0:T(8,128)(2,1)S(1)}, u32[]{:S(2)}, u32[]{:S(2)}) collective-permute-start(bf16[128,1280]{1,0:T(8,128)(2,1)S(1)} %get-tuple-element.30), channel_id=1, source_target_pairs={{0,1},{1,0},{2,3},{3,2},{4,5},{5,4},{6,7},{7,6},{8,9},{9,8},{10,11... | collective-permute-start | bytes 983048 | tf_op jit(solution)/shard_map/ppermute | solution.py:29
  74.2 3.2 %collective-permute-start.16 = (bf16[128,1280]{1,0:T(8,128)(2,1)S(1)}, bf16[128,1280]{1,0:T(8,128)(2,1)S(1)}, u32[]{:S(2)}, u32[]{:S(2)}) collective-permute-start(bf16[128,1280]{1,0:T(8,128)(2,1)S(1)} %get-tuple-element.29), channel_id=1, source_target_pairs={{0,1},{1,0},{2,3},{3,2},{4,5},{5,4},{6,7},{7,6},{8,9},{9,8},{10,11... | collective-permute-start | bytes 983048 | tf_op jit(solution)/shard_map/ppermute | solution.py:29
  74.3 3.1 %collective-permute-start.7 = (bf16[128,1280]{1,0:T(8,128)(2,1)S(1)}, bf16[128,1280]{1,0:T(8,128)(2,1)S(1)}, u32[]{:S(2)}, u32[]{:S(2)}) collective-permute-start(bf16[128,1280]{1,0:T(8,128)(2,1)S(1)} %get-tuple-element.28), channel_id=1, source_target_pairs={{0,1},{1,0},{2,3},{3,2},{4,5},{5,4},{6,7},{7,6},{8,9},{9,8},{10,11... | collective-permute-start | bytes 983048 | tf_op jit(solution)/shard_map/ppermute | solution.py:29
  76.0 7.7 %collective-permute-start.6 = (bf16[128,1280]{1,0:T(8,128)(2,1)S(1)}, bf16[128,1280]{1,0:T(8,128)(2,1)S(1)}, u32[]{:S(2)}, u32[]{:S(2)}) collective-permute-start(bf16[128,1280]{1,0:T(8,128)(2,1)S(1)} %get-tuple-element.23), channel_id=1, source_target_pairs={{0,1},{1,0},{2,3},{3,2},{4,5},{5,4},{6,7},{7,6},{8,9},{9,8},{10,11... | collective-permute-start | bytes 983048 | tf_op jit(solution)/shard_map/ppermute | solution.py:29
  78.6 10.8 %collective-permute-start.8 = (bf16[128,1280]{1,0:T(8,128)(2,1)}, bf16[128,1280]{1,0:T(8,128)(2,1)S(1)}, u32[]{:S(2)}, u32[]{:S(2)}) collective-permute-start(bf16[128,1280]{1,0:T(8,128)(2,1)} %get-tuple-element.24), channel_id=1, source_target_pairs={{0,2},{1,3},{2,0},{3,1},{4,6},{5,7},{6,4},{7,5},{8,10},{9,11},{10,... | collective-permute-start | bytes 983048 | tf_op jit(solution)/shard_map/ppermute | solution.py:29
  80.3 17.6 %collective-permute-start.9 = (bf16[128,1280]{1,0:T(8,128)(2,1)S(1)}, bf16[128,1280]{1,0:T(8,128)(2,1)S(1)}, u32[]{:S(2)}, u32[]{:S(2)}) collective-permute-start(bf16[128,1280]{1,0:T(8,128)(2,1)S(1)} %get-tuple-element.22), channel_id=1, source_target_pairs={{0,1},{1,0},{2,3},{3,2},{4,5},{5,4},{6,7},{7,6},{8,9},{9,8},{10,11... | collective-permute-start | bytes 983048 | tf_op jit(solution)/shard_map/ppermute | solution.py:29
  80.6 22.8 %collective-permute-start.12 = (bf16[128,1280]{1,0:T(8,128)(2,1)S(1)}, bf16[128,1280]{1,0:T(8,128)(2,1)S(1)}, u32[]{:S(2)}, u32[]{:S(2)}) collective-permute-start(bf16[128,1280]{1,0:T(8,128)(2,1)S(1)} %get-tuple-element.21), channel_id=1, source_target_pairs={{0,1},{1,0},{2,3},{3,2},{4,5},{5,4},{6,7},{7,6},{8,9},{9,8},{10,11... | collective-permute-start | bytes 983048 | tf_op jit(solution)/shard_map/ppermute | solution.py:29
  80.9 2.9 %copy-start.6 = (bf16[128,1280]{1,0:T(8,128)(2,1)S(1)}, bf16[128,1280]{1,0:T(8,128)(2,1)}, u32[]{:S(2)}) copy-start(bf16[128,1280]{1,0:T(8,128)(2,1)} %get-tuple-element.27) | copy-start | bytes 983044
  80.9 10.0 %copy-start.5 = (bf16[512,1280]{1,0:T(8,128)(2,1)S(1)}, bf16[512,1280]{1,0:T(8,128)(2,1)}, u32[]{:S(2)}) copy-start(bf16[512,1280]{1,0:T(8,128)(2,1)} %param.9) | copy-start | bytes 3932164
  80.9 29.0 %collective-permute-start.15 = (bf16[128,1280]{1,0:T(8,128)(2,1)S(1)}, bf16[128,1280]{1,0:T(8,128)(2,1)S(1)}, u32[]{:S(2)}, u32[]{:S(2)}) collective-permute-start(bf16[128,1280]{1,0:T(8,128)(2,1)S(1)} %get-tuple-element.20), channel_id=1, source_target_pairs={{0,1},{1,0},{2,3},{3,2},{4,5},{5,4},{6,7},{7,6},{8,9},{9,8},{10,11... | collective-permute-start | bytes 983048 | tf_op jit(solution)/shard_map/ppermute | solution.py:29
  83.8 12.6 %collective-permute-start.11 = (bf16[128,1280]{1,0:T(8,128)(2,1)S(1)}, bf16[128,1280]{1,0:T(8,128)(2,1)S(1)}, u32[]{:S(2)}, u32[]{:S(2)}) collective-permute-start(bf16[128,1280]{1,0:T(8,128)(2,1)S(1)} %copy-done.6), channel_id=1, source_target_pairs={{0,2},{1,3},{2,0},{3,1},{4,6},{5,7},{6,4},{7,5},{8,10},{9,11},{10,... | collective-permute-start | bytes 983048 | tf_op jit(solution)/shard_map/ppermute | solution.py:29
  89.4 14.0 %collective-permute-start.14 = (bf16[128,1280]{1,0:T(8,128)(2,1)S(1)}, bf16[128,1280]{1,0:T(8,128)(2,1)S(1)}, u32[]{:S(2)}, u32[]{:S(2)}) collective-permute-start(bf16[128,1280]{1,0:T(8,128)(2,1)S(1)} %get-tuple-element.26), channel_id=1, source_target_pairs={{0,2},{1,3},{2,0},{3,1},{4,6},{5,7},{6,4},{7,5},{8,10},{9,11},{10,... | collective-permute-start | bytes 983048 | tf_op jit(solution)/shard_map/ppermute | solution.py:29
  96.4 13.5 %collective-permute-start.17 = (bf16[128,1280]{1,0:T(8,128)(2,1)S(1)}, bf16[128,1280]{1,0:T(8,128)(2,1)S(1)}, u32[]{:S(2)}, u32[]{:S(2)}) collective-permute-start(bf16[128,1280]{1,0:T(8,128)(2,1)S(1)} %get-tuple-element.25), channel_id=1, source_target_pairs={{0,2},{1,3},{2,0},{3,1},{4,6},{5,7},{6,4},{7,5},{8,10},{9,11},{10,... | collective-permute-start | bytes 983048 | tf_op jit(solution)/shard_map/ppermute | solution.py:29
  110.9 32.6 %copy-start.4 = (bf16[512,1280]{1,0:T(8,128)(2,1)S(1)}, bf16[512,1280]{1,0:T(8,128)(2,1)}, u32[]{:S(2)}) copy-start(bf16[512,1280]{1,0:T(8,128)(2,1)} %param.17) | copy-start | bytes 3932164
  110.9 12.8 %collective-permute-start.21 = (bf16[128,1280]{1,0:T(8,128)(2,1)}, bf16[128,1280]{1,0:T(8,128)(2,1)S(1)}, u32[]{:S(2)}, u32[]{:S(2)}) collective-permute-start(bf16[128,1280]{1,0:T(8,128)(2,1)} %get-tuple-element.12), channel_id=1, source_target_pairs={{4,0},{8,4},{12,8},{16,12},{20,16},{24,20},{28,24},{5,1},{9,5},{13... | collective-permute-start | bytes 983048 | tf_op jit(solution)/shard_map/ppermute | solution.py:24
  112.3 18.4 %collective-permute-start.20 = (bf16[128,1280]{1,0:T(8,128)(2,1)}, bf16[128,1280]{1,0:T(8,128)(2,1)S(1)}, u32[]{:S(2)}, u32[]{:S(2)}) collective-permute-start(bf16[128,1280]{1,0:T(8,128)(2,1)} %get-tuple-element.19), channel_id=1, source_target_pairs={{4,0},{8,4},{12,8},{16,12},{20,16},{24,20},{28,24},{5,1},{9,5},{13... | collective-permute-start | bytes 983048 | tf_op jit(solution)/shard_map/ppermute | solution.py:24
  113.6 24.2 %collective-permute-start.19 = (bf16[128,1280]{1,0:T(8,128)(2,1)}, bf16[128,1280]{1,0:T(8,128)(2,1)}, u32[]{:S(2)}, u32[]{:S(2)}) collective-permute-start(bf16[128,1280]{1,0:T(8,128)(2,1)} %get-tuple-element.17), channel_id=1, source_target_pairs={{4,0},{8,4},{12,8},{16,12},{20,16},{24,20},{28,24},{5,1},{9,5},{13... | collective-permute-start | bytes 983048 | tf_op jit(solution)/shard_map/ppermute | solution.py:24
  114.9 28.6 %collective-permute-start.18 = (bf16[128,1280]{1,0:T(8,128)(2,1)}, bf16[128,1280]{1,0:T(8,128)(2,1)}, u32[]{:S(2)}, u32[]{:S(2)}) collective-permute-start(bf16[128,1280]{1,0:T(8,128)(2,1)} %get-tuple-element.15), channel_id=1, source_target_pairs={{4,0},{8,4},{12,8},{16,12},{20,16},{24,20},{28,24},{5,1},{9,5},{13... | collective-permute-start | bytes 983048 | tf_op jit(solution)/shard_map/ppermute | solution.py:24

commit v2 on v1

--- a/solution.py
+++ b/solution.py
@@ -11,7 +11,7 @@
 
 HD = 128
 LEVELS = 4
-CHUNKS = 4
+CUTS = (0, 10, 19, 27, 32)
 MASKED = -1e30
 
 
@@ -137,9 +137,8 @@
     out_width = latents.shape[1]
     heads = lax.axis_size("head")
     me = lax.axis_index("head")
-    step = rows // CHUNKS
     bf16 = jnp.bfloat16
-    parts = [slice(chunk * step, (chunk + 1) * step) for chunk in range(CHUNKS)]
+    parts = [slice(rows * low // 32, rows * high // 32) for low, high in zip(CUTS, CUTS[1:])]
 
     def project(owner):
         weight = lax.dynamic_slice_in_dim(out_weight, owner * out_width, out_width, 1)
@@ -147,12 +146,14 @@
 
     if heads == 4:
         for_pair = project(me ^ 3)
-        from_pair = [swapped(for_pair[here], "head", 1) for here in parts]
+        from_pair = []
+        for here in parts:
+            from_pair.append(swapped(for_pair[here], "head", 1))
         for_far = project(me ^ 2)
-        from_far = [
-            swapped((for_far[here].astype(f32) + from_pair[chunk].astype(f32)).astype(bf16), "head", 2)
-            for chunk, here in enumerate(parts)
-        ]
+        from_far = []
+        for chunk, here in enumerate(parts):
+            both = (for_far[here].astype(f32) + from_pair[chunk].astype(f32)).astype(bf16)
+            from_far.append(swapped(both, "head", 2))
         for_near = project(me ^ 1)
         from_near = [swapped(for_near[here], "head", 1) for here in parts]
         own = project(me)
@@ -174,7 +175,11 @@
         updated = (latents[here].astype(f32) + delta * gated).astype(bf16)
         moves.append(shifted(updated, "frame", -1))
         before = updated
-    next_latents = jnp.where(is_last, fresh, jnp.concatenate(moves, 0))
+    final = parts[-1]
+    most = jnp.where(is_last, fresh, jnp.concatenate(moves[:-1] + [fresh[final]], 0))
+    most = lax.optimization_barrier(most)
+    rest = jnp.where(is_last, fresh[final], moves[-1])
+    next_latents = lax.dynamic_update_slice(most, rest, (final.start, 0))
     return (jnp.concatenate(velocities, 0), next_latents)
 
 

time: 146 us -> 138 us (0.945)
  other arithmetic: 10.7 us -> 4.86 us
  waiting for transfers between devices: 77.7 us -> 75.6 us
  matrix products: 8.07 us -> 6.56 us
    ppermute x8, waiting for transfers between devices: 49.2 us -> 41.5 us  [shifted(): return lax.ppermute(value, axis, pairs)]
    ppermute x14, waiting for transfers between devices: 28.5 us -> 34.1 us  [swapped(): return lax.ppermute(value, axis, [(i, i ^ bit) for i in range(devices)])]
    convert_element_type x3, other arithmetic: 2.9 us -> 0.78 us  [shards(): velocities.append(gated.astype(bf16))]
    select_n x1, other arithmetic: 2.44 us -> 0.33 us  [shards(): jnp.where(is_last, fresh, jnp.concatenate(moves[:-1] + [fresh[final]], 0))]
    dot_general x4, matrix products: 7.91 us -> 6.4 us  [project(): return jnp.dot(attended, weight, preferred_element_type=f32).astype(bf16)]
  transfers between devices with their start and end apart: 22 -> 22, of which waited for: 12 -> 9; matrix products, arithmetic and copies ran while one was open for 9% -> 5% of each run, Pallas kernels for 9% -> 10%
where the time goes in v2:
time: 138 us
  waiting for transfers between devices  75.6 us (55%)
  starting transfers between devices  32.6 us (24%)
  Pallas kernels  15.3 us (11%)
  matrix products  6.56 us (5%)
  other arithmetic  4.86 us (4%)
  between operations  1.86 us (1%)
    ppermute x8, waiting for transfers between devices, shifted(): return lax.ppermute(value, axis, pairs)  41.5 us
    ppermute x14, waiting for transfers between devices, swapped(): return lax.ppermute(value, axis, [(i, i ^ bit) for i in range(devices)])  34.1 us
    ppermute x8, starting transfers between devices, shifted(): return lax.ppermute(value, axis, pairs)  23.1 us
    pallas_call x1, Pallas kernels, attention(): pl.pallas_call(functools.partial(weights_kernel, blocks), grid=(heads,),...  13.5 us
    ppermute x14, starting transfers between devices, swapped(): return lax.ppermute(value, axis, [(i, i ^ bit) for i in range(devices)])  9.56 us
    dot_general x4, matrix products, project(): return jnp.dot(attended, weight, preferred_element_type=f32).astype(bf16)  6.4 us
  transfers between devices with their start and end apart: 22, of which 9 were waited for; matrix products, arithmetic and copies ran while one was open for 5% of the time, Pallas kernels for 10%

profile of v2, /device:TPU:0, one launch (start us, length us, event | category | flops | bytes accessed | tf_op | source)
XLA Modules:
  0.0 138.1 jit_solution(12283147052122341393)
XLA Ops:
  0.7 5.1 %collective-permute-start = (bf16[512,640]{1,0:T(8,128)(2,1)}, bf16[512,640]{1,0:T(8,128)(2,1)S(1)}, u32[]{:S(2)}, u32[]{:S(2)}) collective-permute-start(bf16[512,640]{1,0:T(8,128)(2,1)} %refs_0_.1), channel_id=1, source_target_pairs={{0,8},{4,12},{8,16},{12,20},{16,24},{20,28},{1,9},{5,13},{9,17},{1... | collective-permute-start | bytes 1966088 | tf_op jit(solution)/shard_map/ppermute | solution.py:24
  5.8 3.5 %collective-permute-start.3 = (bf16[512,640]{1,0:T(8,128)(2,1)}, bf16[512,640]{1,0:T(8,128)(2,1)S(1)}, u32[]{:S(2)}, u32[]{:S(2)}) collective-permute-start(bf16[512,640]{1,0:T(8,128)(2,1)} %refs_4_.1), channel_id=1, source_target_pairs={{0,8},{4,12},{8,16},{12,20},{16,24},{20,28},{1,9},{5,13},{9,17},{1... | collective-permute-start | bytes 1966088 | tf_op jit(solution)/shard_map/ppermute | solution.py:24
  9.3 11.9 %collective-permute-done.refs_2_ = bf16[512,640]{1,0:T(8,128)(2,1)S(1)} collective-permute-done((bf16[512,640]{1,0:T(8,128)(2,1)}, bf16[512,640]{1,0:T(8,128)(2,1)S(1)}, u32[]{:S(2)}, u32[]{:S(2)}) %collective-permute-start) | collective-permute-done | bytes 655392 | tf_op jit(solution)/shard_map/ppermute | solution.py:24
  21.2 1.2 broadcast_select_fusion.1
  22.4 0.5 collective-permute-start.1
  22.9 11.2 %collective-permute-done.3.refs_6_ = bf16[512,640]{1,0:T(8,128)(2,1)S(1)} collective-permute-done((bf16[512,640]{1,0:T(8,128)(2,1)}, bf16[512,640]{1,0:T(8,128)(2,1)S(1)}, u32[]{:S(2)}, u32[]{:S(2)}) %collective-permute-start.3) | collective-permute-done | bytes 655392 | tf_op jit(solution)/shard_map/ppermute | solution.py:24
  34.1 0.9 broadcast_select_fusion
  35.0 1.5 %collective-permute-start.4 = (bf16[512,640]{1,0:T(8,128)(2,1)}, bf16[512,640]{1,0:T(8,128)(2,1)}, u32[]{:S(2)}, u32[]{:S(2)}) collective-permute-start(bf16[512,640]{1,0:T(8,128)(2,1)} %broadcast_select_fusion), channel_id=1, source_target_pairs={{0,4},{4,0},{8,12},{12,8},{16,20},{20,16},{24,28},{28,24},{1,5},{5... | collective-permute-start | bytes 1966088 | tf_op jit(solution)/shard_map/ppermute | solution.py:29
  36.5 0.6 collective-permute-done.1.refs_1_
  37.2 5.0 %collective-permute-start.2 = (bf16[512,640]{1,0:T(8,128)(2,1)}, bf16[512,640]{1,0:T(8,128)(2,1)}, u32[]{:S(2)}, u32[]{:S(2)}) collective-permute-start(bf16[512,640]{1,0:T(8,128)(2,1)} %collective-permute-done.1.refs_1_), channel_id=1, source_target_pairs={{0,8},{4,12},{8,16},{12,20},{16,24},{20,28},{1,9},{5,13},{9,17},{1... | collective-permute-start | bytes 1966088 | tf_op jit(solution)/shard_map/ppermute | solution.py:24
  42.9 0.2 convolution_reduce_fusion
  43.1 8.0 %collective-permute-done.4.refs_5_ = bf16[512,640]{1,0:T(8,128)(2,1)} collective-permute-done((bf16[512,640]{1,0:T(8,128)(2,1)}, bf16[512,640]{1,0:T(8,128)(2,1)}, u32[]{:S(2)}, u32[]{:S(2)}) %collective-permute-start.4) | collective-permute-done | bytes 655392 | tf_op jit(solution)/shard_map/ppermute | solution.py:29
  51.1 4.3 %collective-permute-start.5 = (bf16[512,640]{1,0:T(8,128)(2,1)}, bf16[512,640]{1,0:T(8,128)(2,1)S(1)}, u32[]{:S(2)}, u32[]{:S(2)}) collective-permute-start(bf16[512,640]{1,0:T(8,128)(2,1)} %collective-permute-done.4.refs_5_), channel_id=1, source_target_pairs={{0,8},{4,12},{8,16},{12,20},{16,24},{20,28},{1,9},{5,13},{9,17},{1... | collective-permute-start | bytes 1966088 | tf_op jit(solution)/shard_map/ppermute | solution.py:24
  55.4 13.5 %shard_map.104 = (f32[512,640]{1,0:T(8,128)S(1)}, bf16[2560,512]{1,0:T(8,128)(2,1)S(1)}) custom-call(s32[4]{0:T(128)S(1)} %fusion.8.flag_ref, bf16[512,640]{1,0:T(8,128)(2,1)S(1)} %copy-done.3, bf16[512,640]{1,0:T(8,128)(2,1)S(1)} %copy-done.1, bf16[512,640]{1,0:T(8,128)(2,1)} %collective-permute-done.1.refs_1_, ...), custom_call_target="tpu_custom_call" | custom-call | flops 10737418240 | bytes 10485760 | tf_op jit(solution)/shard_map/pallas_call | solution.py:73
  68.9 1.8 %shard_map.105 = bf16[512,640]{1,0:T(8,128)(2,1)S(1)} custom-call(bf16[2560,512]{1,0:T(8,128)(2,1)S(1)} %get-tuple-element.7.weight_ref, bf16[512,640]{1,0:T(8,128)(2,1)S(1)} %collective-permute-done.5.v_ref, f32[512,640]{1,0:T(8,128)S(1)} %get-tuple-element.8.acc_ref), custom_call_target="tpu_custom_call" | custom-call | flops 335544320 | bytes 2621440 | tf_op jit(solution)/shard_map/pallas_call | solution.py:89
  70.8 2.8 %convolution_convert_fusion = bf16[512,1280]{1,0:T(8,128)(2,1)S(1)} fusion(bf16[512,640]{1,0:T(8,128)(2,1)S(1)} %shard_map.105, bf16[640,5120]{1,0:T(8,128)(2,1)} %param.13, s32[]{:T(128)S(6)} %select_n.54), kind=kOutput, calls=%fused_computation | convolution fusion | flops 839516160 | bytes 3604484 | tf_op jit(solution)/shard_map/dot_general | solution.py:145
  73.7 1.2 convolution_convert_fusion.2
  75.1 1.2 convolution_convert_fusion.1
  76.4 0.6 collective-permute-start.13
  76.9 0.1 collective-permute-start.10
  77.0 0.4 collective-permute-start.7
  77.5 1.2 convolution_convert_fusion.3
  78.7 0.5 collective-permute-start.9
  79.3 0.1 collective-permute-start.12
  79.4 0.1 add_convert_fusion.5
  79.5 0.5 collective-permute-start.15
  80.1 0.1 add_convert_fusion.1
  80.2 1.6 %collective-permute-start.8 = (bf16[160,1280]{1,0:T(8,128)(2,1)S(1)}, bf16[160,1280]{1,0:T(8,128)(2,1)S(1)}, u32[]{:S(2)}, u32[]{:S(2)}) collective-permute-start(bf16[160,1280]{1,0:T(8,128)(2,1)S(1)} %add_convert_fusion.1), channel_id=1, source_target_pairs={{0,2},{1,3},{2,0},{3,1},{4,6},{5,7},{6,4},{7,5},{8,10},{9,11},{10,... | collective-permute-start | bytes 1228808 | tf_op jit(solution)/shard_map/ppermute | solution.py:29
  81.7 0.1 add_convert_fusion.3
  81.8 0.6 collective-permute-start.17
  82.4 10.1 %collective-permute-done.8 = bf16[160,1280]{1,0:T(8,128)(2,1)S(1)} collective-permute-done((bf16[160,1280]{1,0:T(8,128)(2,1)S(1)}, bf16[160,1280]{1,0:T(8,128)(2,1)S(1)}, u32[]{:S(2)}, u32[]{:S(2)}) %collective-permute-start.8) | collective-permute-done | bytes 409632 | tf_op jit(solution)/shard_map/ppermute | solution.py:29
  92.6 1.5 %collective-permute-start.11 = (bf16[144,1280]{1,0:T(8,128)(2,1)S(1)}, bf16[144,1280]{1,0:T(8,128)(2,1)S(1)}, u32[]{:S(2)}, u32[]{:S(2)}) collective-permute-start(bf16[144,1280]{1,0:T(8,128)(2,1)S(1)} %add_convert_fusion.3), channel_id=1, source_target_pairs={{0,2},{1,3},{2,0},{3,1},{4,6},{5,7},{6,4},{7,5},{8,10},{9,11},{10,... | collective-permute-start | bytes 1105928 | tf_op jit(solution)/shard_map/ppermute | solution.py:29
  94.1 0.3 fusion.4
  94.3 9.6 %collective-permute-done.11 = bf16[144,1280]{1,0:T(8,128)(2,1)S(1)} collective-permute-done((bf16[144,1280]{1,0:T(8,128)(2,1)S(1)}, bf16[144,1280]{1,0:T(8,128)(2,1)S(1)}, u32[]{:S(2)}, u32[]{:S(2)}) %collective-permute-start.11) | collective-permute-done | bytes 368672 | tf_op jit(solution)/shard_map/ppermute | solution.py:29
  103.9 1.5 %collective-permute-start.14 = (bf16[128,1280]{1,0:T(8,128)(2,1)S(1)}, bf16[128,1280]{1,0:T(8,128)(2,1)S(1)}, u32[]{:S(2)}, u32[]{:S(2)}) collective-permute-start(bf16[128,1280]{1,0:T(8,128)(2,1)S(1)} %add_convert_fusion.5), channel_id=1, source_target_pairs={{0,2},{1,3},{2,0},{3,1},{4,6},{5,7},{6,4},{7,5},{8,10},{9,11},{10,... | collective-permute-start | bytes 983048 | tf_op jit(solution)/shard_map/ppermute | solution.py:29
  105.5 1.3 collective-permute-start.18
  106.8 0.3 fusion.5
  107.0 5.7 %collective-permute-done.14 = bf16[128,1280]{1,0:T(8,128)(2,1)S(1)} collective-permute-done((bf16[128,1280]{1,0:T(8,128)(2,1)S(1)}, bf16[128,1280]{1,0:T(8,128)(2,1)S(1)}, u32[]{:S(2)}, u32[]{:S(2)}) %collective-permute-start.14) | collective-permute-done | bytes 327712 | tf_op jit(solution)/shard_map/ppermute | solution.py:29
  112.8 1.3 collective-permute-start.19
  114.1 0.2 fusion.6
  114.3 1.3 collective-permute-start.20
  115.6 0.1 add_convert_fusion.6
  115.8 1.3 collective-permute-start.21
  117.1 1.1 pad_maximum_fusion
  118.2 16.4 %collective-permute-done.20 = bf16[128,1280]{1,0:T(8,128)(2,1)S(1)} collective-permute-done((bf16[128,1280]{1,0:T(8,128)(2,1)S(1)}, bf16[128,1280]{1,0:T(8,128)(2,1)S(1)}, u32[]{:S(2)}, u32[]{:S(2)}) %collective-permute-start.20) | collective-permute-done | bytes 327712 | tf_op jit(solution)/shard_map/ppermute | solution.py:24
  134.6 0.3 maximum_select_fusion
  135.0 2.0 %collective-permute-done.21 = bf16[80,1280]{1,0:T(8,128)(2,1)S(1)} collective-permute-done((bf16[80,1280]{1,0:T(8,128)(2,1)S(1)}, bf16[80,1280]{1,0:T(8,128)(2,1)S(1)}, u32[]{:S(2)}, u32[]{:S(2)}) %collective-permute-start.21) | collective-permute-done | bytes 204832 | tf_op jit(solution)/shard_map/ppermute | solution.py:24
  137.0 1.0 copy-done.6
  (48 shorter events, 0.5 us)
Async XLA Ops:
  0.6 42.3 %copy-start = (f32[4,1280]{1,0:T(4,128)S(1)}, f32[4,1280]{1,0:T(4,128)}, u32[]{:S(2)}) copy-start(f32[4,1280]{1,0:T(4,128)} %param.14) | copy-start | bytes 61444
  0.6 33.4 %copy-start.2 = (bf16[512,640]{1,0:T(8,128)(2,1)S(1)}, bf16[512,640]{1,0:T(8,128)(2,1)}, u32[]{:S(2)}) copy-start(bf16[512,640]{1,0:T(8,128)(2,1)} %refs_4_.1) | copy-start | bytes 1966084
  0.7 20.5 %collective-permute-start = (bf16[512,640]{1,0:T(8,128)(2,1)}, bf16[512,640]{1,0:T(8,128)(2,1)S(1)}, u32[]{:S(2)}, u32[]{:S(2)}) collective-permute-start(bf16[512,640]{1,0:T(8,128)(2,1)} %refs_0_.1), channel_id=1, source_target_pairs={{0,8},{4,12},{8,16},{12,20},{16,24},{20,28},{1,9},{5,13},{9,17},{1... | collective-permute-start | bytes 1966088 | tf_op jit(solution)/shard_map/ppermute | solution.py:24
  5.8 28.3 %collective-permute-start.3 = (bf16[512,640]{1,0:T(8,128)(2,1)}, bf16[512,640]{1,0:T(8,128)(2,1)S(1)}, u32[]{:S(2)}, u32[]{:S(2)}) collective-permute-start(bf16[512,640]{1,0:T(8,128)(2,1)} %refs_4_.1), channel_id=1, source_target_pairs={{0,8},{4,12},{8,16},{12,20},{16,24},{20,28},{1,9},{5,13},{9,17},{1... | collective-permute-start | bytes 1966088 | tf_op jit(solution)/shard_map/ppermute | solution.py:24
  22.3 20.8 %copy-start.7 = (s32[1,4]{1,0:T(1,128)S(1)}, s32[1,4]{1,0:T(1,128)}, u32[]{:S(2)}) copy-start(s32[1,4]{1,0:T(1,128)} %param.16) | copy-start | bytes 52
  22.3 33.1 %copy-start.1 = (bf16[512,640]{1,0:T(8,128)(2,1)S(1)}, bf16[512,640]{1,0:T(8,128)(2,1)}, u32[]{:S(2)}) copy-start(bf16[512,640]{1,0:T(8,128)(2,1)} %refs_0_.1) | copy-start | bytes 1966084
  22.4 33.1 %copy-start.3 = (bf16[512,640]{1,0:T(8,128)(2,1)S(1)}, bf16[512,640]{1,0:T(8,128)(2,1)}, u32[]{:S(2)}) copy-start(bf16[512,640]{1,0:T(8,128)(2,1)} %q_ref.1) | copy-start | bytes 1966084
  22.4 14.8 %collective-permute-start.1 = (bf16[512,640]{1,0:T(8,128)(2,1)S(1)}, bf16[512,640]{1,0:T(8,128)(2,1)}, u32[]{:S(2)}, u32[]{:S(2)}) collective-permute-start(bf16[512,640]{1,0:T(8,128)(2,1)S(1)} %broadcast_select_fusion.1), channel_id=1, source_target_pairs={{0,4},{4,0},{8,12},{12,8},{16,20},{20,16},{24,28},{28,24},{1,5},{5... | collective-permute-start | bytes 1966088 | tf_op jit(solution)/shard_map/ppermute | solution.py:29
  35.0 16.1 %collective-permute-start.4 = (bf16[512,640]{1,0:T(8,128)(2,1)}, bf16[512,640]{1,0:T(8,128)(2,1)}, u32[]{:S(2)}, u32[]{:S(2)}) collective-permute-start(bf16[512,640]{1,0:T(8,128)(2,1)} %broadcast_select_fusion), channel_id=1, source_target_pairs={{0,4},{4,0},{8,12},{12,8},{16,20},{20,16},{24,28},{28,24},{1,5},{5... | collective-permute-start | bytes 1966088 | tf_op jit(solution)/shard_map/ppermute | solution.py:29
  37.2 18.2 %collective-permute-start.2 = (bf16[512,640]{1,0:T(8,128)(2,1)}, bf16[512,640]{1,0:T(8,128)(2,1)}, u32[]{:S(2)}, u32[]{:S(2)}) collective-permute-start(bf16[512,640]{1,0:T(8,128)(2,1)} %collective-permute-done.1.refs_1_), channel_id=1, source_target_pairs={{0,8},{4,12},{8,16},{12,20},{16,24},{20,28},{1,9},{5,13},{9,17},{1... | collective-permute-start | bytes 1966088 | tf_op jit(solution)/shard_map/ppermute | solution.py:24
  51.1 17.8 %collective-permute-start.5 = (bf16[512,640]{1,0:T(8,128)(2,1)}, bf16[512,640]{1,0:T(8,128)(2,1)S(1)}, u32[]{:S(2)}, u32[]{:S(2)}) collective-permute-start(bf16[512,640]{1,0:T(8,128)(2,1)} %collective-permute-done.4.refs_5_), channel_id=1, source_target_pairs={{0,8},{4,12},{8,16},{12,20},{16,24},{20,28},{1,9},{5,13},{9,17},{1... | collective-permute-start | bytes 1966088 | tf_op jit(solution)/shard_map/ppermute | solution.py:24
  68.9 4.8 %slice-start.1 = ((s8[6553600]{0:T(1024)(128)(4,1)}), s8[2359296]{0:T(1024)(128)(4,1)S(1)}, s32[]{:S(2)}) async-start(s8[6553600]{0:T(1024)(128)(4,1)} %bitcast.15), calls=%async_computation.1 | async-start | bytes 4718592
  70.8 2.9 %slice-start.2 = ((s8[6553600]{0:T(1024)(128)(4,1)}), s8[4194304]{0:T(1024)(128)(4,1)S(1)}, s32[]{:S(2)}) async-start(s8[6553600]{0:T(1024)(128)(4,1)} %bitcast.15), calls=%async_computation.2 | async-start | bytes 8388608
  75.0 3.6 %collective-permute-start.16 = (bf16[80,1280]{1,0:T(8,128)(2,1)S(1)}, bf16[80,1280]{1,0:T(8,128)(2,1)S(1)}, u32[]{:S(2)}, u32[]{:S(2)}) collective-permute-start(bf16[80,1280]{1,0:T(8,128)(2,1)S(1)} %slice.100), channel_id=1, source_target_pairs={{0,1},{1,0},{2,3},{3,2},{4,5},{5,4},{6,7},{7,6},{8,9},{9,8},{10,11... | collective-permute-start | bytes 614408 | tf_op jit(solution)/shard_map/ppermute | solution.py:29
  76.4 2.9 %collective-permute-start.13 = (bf16[128,1280]{1,0:T(8,128)(2,1)S(1)}, bf16[128,1280]{1,0:T(8,128)(2,1)S(1)}, u32[]{:S(2)}, u32[]{:S(2)}) collective-permute-start(bf16[128,1280]{1,0:T(8,128)(2,1)S(1)} %slice.96), channel_id=1, source_target_pairs={{0,1},{1,0},{2,3},{3,2},{4,5},{5,4},{6,7},{7,6},{8,9},{9,8},{10,11... | collective-permute-start | bytes 983048 | tf_op jit(solution)/shard_map/ppermute | solution.py:29
  76.9 3.3 %collective-permute-start.10 = (bf16[144,1280]{1,0:T(8,128)(2,1)S(1)}, bf16[144,1280]{1,0:T(8,128)(2,1)S(1)}, u32[]{:S(2)}, u32[]{:S(2)}) collective-permute-start(bf16[144,1280]{1,0:T(8,128)(2,1)S(1)} %slice.92), channel_id=1, source_target_pairs={{0,1},{1,0},{2,3},{3,2},{4,5},{5,4},{6,7},{7,6},{8,9},{9,8},{10,11... | collective-permute-start | bytes 1105928 | tf_op jit(solution)/shard_map/ppermute | solution.py:29
  77.0 2.5 %collective-permute-start.7 = (bf16[160,1280]{1,0:T(8,128)(2,1)S(1)}, bf16[160,1280]{1,0:T(8,128)(2,1)S(1)}, u32[]{:S(2)}, u32[]{:S(2)}) collective-permute-start(bf16[160,1280]{1,0:T(8,128)(2,1)S(1)} %slice.88), channel_id=1, source_target_pairs={{0,1},{1,0},{2,3},{3,2},{4,5},{5,4},{6,7},{7,6},{8,9},{9,8},{10,11... | collective-permute-start | bytes 1228808 | tf_op jit(solution)/shard_map/ppermute | solution.py:29
  77.4 4.4 %collective-permute-start.6 = (bf16[160,1280]{1,0:T(8,128)(2,1)S(1)}, bf16[160,1280]{1,0:T(8,128)(2,1)S(1)}, u32[]{:S(2)}, u32[]{:S(2)}) collective-permute-start(bf16[160,1280]{1,0:T(8,128)(2,1)S(1)} %slice.86), channel_id=1, source_target_pairs={{0,1},{1,0},{2,3},{3,2},{4,5},{5,4},{6,7},{7,6},{8,9},{9,8},{10,11... | collective-permute-start | bytes 1228808 | tf_op jit(solution)/shard_map/ppermute | solution.py:29
  78.7 26.8 %collective-permute-start.9 = (bf16[144,1280]{1,0:T(8,128)(2,1)S(1)}, bf16[144,1280]{1,0:T(8,128)(2,1)S(1)}, u32[]{:S(2)}, u32[]{:S(2)}) collective-permute-start(bf16[144,1280]{1,0:T(8,128)(2,1)S(1)} %slice.90), channel_id=1, source_target_pairs={{0,1},{1,0},{2,3},{3,2},{4,5},{5,4},{6,7},{7,6},{8,9},{9,8},{10,11... | collective-permute-start | bytes 1105928 | tf_op jit(solution)/shard_map/ppermute | solution.py:29
  79.3 34.8 %collective-permute-start.12 = (bf16[128,1280]{1,0:T(8,128)(2,1)S(1)}, bf16[128,1280]{1,0:T(8,128)(2,1)S(1)}, u32[]{:S(2)}, u32[]{:S(2)}) collective-permute-start(bf16[128,1280]{1,0:T(8,128)(2,1)S(1)} %slice.94), channel_id=1, source_target_pairs={{0,1},{1,0},{2,3},{3,2},{4,5},{5,4},{6,7},{7,6},{8,9},{9,8},{10,11... | collective-permute-start | bytes 983048 | tf_op jit(solution)/shard_map/ppermute | solution.py:29
  79.5 14.6 %copy-start.5 = (bf16[512,1280]{1,0:T(8,128)(2,1)S(1)}, bf16[512,1280]{1,0:T(8,128)(2,1)}, u32[]{:S(2)}) copy-start(bf16[512,1280]{1,0:T(8,128)(2,1)} %param.9) | copy-start | bytes 3932164
  79.5 36.1 %collective-permute-start.15 = (bf16[80,1280]{1,0:T(8,128)(2,1)S(1)}, bf16[80,1280]{1,0:T(8,128)(2,1)S(1)}, u32[]{:S(2)}, u32[]{:S(2)}) collective-permute-start(bf16[80,1280]{1,0:T(8,128)(2,1)S(1)} %slice.98), channel_id=1, source_target_pairs={{0,1},{1,0},{2,3},{3,2},{4,5},{5,4},{6,7},{7,6},{8,9},{9,8},{10,11... | collective-permute-start | bytes 614408 | tf_op jit(solution)/shard_map/ppermute | solution.py:29
  80.2 12.4 %collective-permute-start.8 = (bf16[160,1280]{1,0:T(8,128)(2,1)S(1)}, bf16[160,1280]{1,0:T(8,128)(2,1)S(1)}, u32[]{:S(2)}, u32[]{:S(2)}) collective-permute-start(bf16[160,1280]{1,0:T(8,128)(2,1)S(1)} %add_convert_fusion.1), channel_id=1, source_target_pairs={{0,2},{1,3},{2,0},{3,1},{4,6},{5,7},{6,4},{7,5},{8,10},{9,11},{10,... | collective-permute-start | bytes 1228808 | tf_op jit(solution)/shard_map/ppermute | solution.py:29
  81.8 33.8 %collective-permute-start.17 = (bf16[80,1280]{1,0:T(8,128)(2,1)S(1)}, bf16[80,1280]{1,0:T(8,128)(2,1)S(1)}, u32[]{:S(2)}, u32[]{:S(2)}) collective-permute-start(bf16[80,1280]{1,0:T(8,128)(2,1)S(1)} %add_convert_fusion.7), channel_id=1, source_target_pairs={{0,2},{1,3},{2,0},{3,1},{4,6},{5,7},{6,4},{7,5},{8,10},{9,11},{10,... | collective-permute-start | bytes 614408 | tf_op jit(solution)/shard_map/ppermute | solution.py:29
  92.6 11.4 %collective-permute-start.11 = (bf16[144,1280]{1,0:T(8,128)(2,1)S(1)}, bf16[144,1280]{1,0:T(8,128)(2,1)S(1)}, u32[]{:S(2)}, u32[]{:S(2)}) collective-permute-start(bf16[144,1280]{1,0:T(8,128)(2,1)S(1)} %add_convert_fusion.3), channel_id=1, source_target_pairs={{0,2},{1,3},{2,0},{3,1},{4,6},{5,7},{6,4},{7,5},{8,10},{9,11},{10,... | collective-permute-start | bytes 1105928 | tf_op jit(solution)/shard_map/ppermute | solution.py:29
  103.9 8.8 %collective-permute-start.14 = (bf16[128,1280]{1,0:T(8,128)(2,1)S(1)}, bf16[128,1280]{1,0:T(8,128)(2,1)S(1)}, u32[]{:S(2)}, u32[]{:S(2)}) collective-permute-start(bf16[128,1280]{1,0:T(8,128)(2,1)S(1)} %add_convert_fusion.5), channel_id=1, source_target_pairs={{0,2},{1,3},{2,0},{3,1},{4,6},{5,7},{6,4},{7,5},{8,10},{9,11},{10,... | collective-permute-start | bytes 983048 | tf_op jit(solution)/shard_map/ppermute | solution.py:29
  105.5 29.1 %collective-permute-start.18 = (bf16[160,1280]{1,0:T(8,128)(2,1)S(1)}, bf16[160,1280]{1,0:T(8,128)(2,1)S(1)}, u32[]{:S(2)}, u32[]{:S(2)}) collective-permute-start(bf16[160,1280]{1,0:T(8,128)(2,1)S(1)} %get-tuple-element.13), channel_id=1, source_target_pairs={{4,0},{8,4},{12,8},{16,12},{20,16},{24,20},{28,24},{5,1},{9,5},{13... | collective-permute-start | bytes 1228808 | tf_op jit(solution)/shard_map/ppermute | solution.py:24
  112.8 21.8 %collective-permute-start.19 = (bf16[144,1280]{1,0:T(8,128)(2,1)S(1)}, bf16[144,1280]{1,0:T(8,128)(2,1)S(1)}, u32[]{:S(2)}, u32[]{:S(2)}) collective-permute-start(bf16[144,1280]{1,0:T(8,128)(2,1)S(1)} %get-tuple-element.15), channel_id=1, source_target_pairs={{4,0},{8,4},{12,8},{16,12},{20,16},{24,20},{28,24},{5,1},{9,5},{13... | collective-permute-start | bytes 1105928 | tf_op jit(solution)/shard_map/ppermute | solution.py:24
  114.3 20.3 %collective-permute-start.20 = (bf16[128,1280]{1,0:T(8,128)(2,1)S(1)}, bf16[128,1280]{1,0:T(8,128)(2,1)S(1)}, u32[]{:S(2)}, u32[]{:S(2)}) collective-permute-start(bf16[128,1280]{1,0:T(8,128)(2,1)S(1)} %get-tuple-element.17), channel_id=1, source_target_pairs={{4,0},{8,4},{12,8},{16,12},{20,16},{24,20},{28,24},{5,1},{9,5},{13... | collective-permute-start | bytes 983048 | tf_op jit(solution)/shard_map/ppermute | solution.py:24
  115.8 21.2 %collective-permute-start.21 = (bf16[80,1280]{1,0:T(8,128)(2,1)S(1)}, bf16[80,1280]{1,0:T(8,128)(2,1)S(1)}, u32[]{:S(2)}, u32[]{:S(2)}) collective-permute-start(bf16[80,1280]{1,0:T(8,128)(2,1)S(1)} %get-tuple-element.18), channel_id=1, source_target_pairs={{4,0},{8,4},{12,8},{16,12},{20,16},{24,20},{28,24},{5,1},{9,5},{13... | collective-permute-start | bytes 614408 | tf_op jit(solution)/shard_map/ppermute | solution.py:24
  117.1 17.5 %copy-start.4 = (bf16[512,1280]{1,0:T(8,128)(2,1)S(1)}, bf16[512,1280]{1,0:T(8,128)(2,1)}, u32[]{:S(2)}) copy-start(bf16[512,1280]{1,0:T(8,128)(2,1)} %param.17) | copy-start | bytes 3932164
  117.1 17.5 %slice-start = ((bf16[512,1280]{1,0:T(8,128)(2,1)}), bf16[80,1280]{1,0:T(8,128)(2,1)S(1)}, s32[]{:S(2)}) async-start(bf16[512,1280]{1,0:T(8,128)(2,1)} %param.17), calls=%async_computation | async-start | bytes 409600 | tf_op jit(solution)/shard_map/slice | solution.py:179
  137.0 1.1 copy-start.6
